TPU v7x, 512 devices: a whole 4x8x8 slice. The times are simulated.
512 devices in a mesh: tm: 8 (over z), lat: 8 (over y_lo, core), lon: 8 (over x, y_hi).
Axes of the slice: x: 4, y: 8 (y_hi: 2, y_lo: 4; y = y_hi * 4 + y_lo), z: 8, core: 2. Of those that a mesh axis runs over, the one named last changes fastest.
Arguments:
- depth_class: int32 [1088, 3072], P('lat', 'lon'), may hold values from 0 to 31
- ocean_mask: int32 [1088, 3072], P('lat', 'lon'), may hold values 0 or 1
- depth_levels: float32 [32], replicated, may hold values from 0.1 to 1
- drag: float32 [1088, 3072], P('lat', 'lon'), may hold values from 0.0005 to 0.02
- tide_force: float32 [2, 1088, 3072], P(None, 'lat', 'lon'), may hold values from -6 to 6
- forward_flow: float32 [4, 1088, 3072], P(None, 'lat', 'lon'), may hold values from -6 to 6
- guess: float32 [8, 3, 1088, 3072], P('tm', None, 'lat', 'lon'), may hold values from -4 to 4
Outputs:
- final_state: float32 [8, 3, 1088, 3072], P('tm', None, 'lat', 'lon')
- drag_gradient: float32 [1088, 3072], P('lat', 'lon')
Inputs may be any that keep to these rules, and one draw needn't show every extreme that they name: `depth_class`: index into depth_levels.
All inputs are finite; a program needn't handle non-finite values. No bound on the sum of `ocean_mask` on one device may be relied on, other than what follows from the above.
Results may differ from a plain program's by a relative error of at most 0.00002.
Values sent between devices are 32-bit elements; how exact they have to be, the bound alone decides.
No kernel may reach another device: no remote copies, remote signals or barrier semaphores. Data moves between devices by JAX's collectives and lax.ppermute only.
A program may use at most 64 MiB of HBM per device.

v0:
```python
import math

import jax
import jax.numpy as jnp
from jax import lax
from jax.sharding import PartitionSpec as P

STEPS = 16
SWEEPS = 2
DCLASS = 32


gravity_coef = 0.7
flux_coef = 0.6


def padded_2(block, sides, width):
    for axis, dim in sides:
        count = lax.axis_size(axis)
        forward = [(i, i + 1) for i in range(count - 1)]
        forward.append((count - 1, 0))
        backward = [(target, source) for source, target in forward]
        low = lax.ppermute(
            lax.slice_in_dim(block, block.shape[dim] - width, None, axis=dim), axis, forward
        )
        high = lax.ppermute(lax.slice_in_dim(block, 0, width, axis=dim), axis, backward)
        block = jnp.concatenate([low, block, high], axis=dim)
    return block


def shifted(value, axis, steps):
    count = lax.axis_size(axis)
    pairs = [(source, (source + steps) % count) for source in range(count)]
    return lax.ppermute(value, axis, pairs)


def carried_in(shard, axis, combine, identity):
    devices, index = (lax.axis_size(axis), lax.axis_index(axis))
    everything = jax.tree.map(lambda part: lax.all_gather(part, axis), shard)
    start = jax.tree.map(
        lambda part, zero: jnp.broadcast_to(jnp.asarray(zero, part.dtype), part.shape),
        shard,
        identity,
    )

    def hop(k, before):
        reached = k < index
        new = combine(before, jax.tree.map(lambda part: part[k], everything))
        return jax.tree.map(lambda a, b: jnp.where(reached, a, b), new, before)

    return lax.fori_loop(0, devices, hop, start)


def from_everyone(shard, axis):
    copies = jnp.broadcast_to(shard, (lax.axis_size(axis), *shard.shape))
    return lax.all_to_all(copies, axis, split_axis=0, concat_axis=0, tiled=True)


def taken_together(shard, axis):
    everything = from_everyone(shard, axis)
    return jnp.sum(everything, axis=0)


def trim(field, margin):
    rows = field.shape[-2]
    cols = field.shape[-1]
    return field[..., margin : rows - margin, margin : cols - margin]


def advance(padded, margin, faces, wide, cosine, sine):
    offset = wide - margin
    depth_u, depth_v, mask_u, mask_v, damp_u, damp_v, mask_c, force_c, force_s = [
        trim(f, offset) for f in faces
    ]
    elev, zonal, merid = (padded[0], padded[1], padded[2])
    zonal_new = mask_u[1:-1, 1:] * (
        damp_u[1:-1, 1:] * zonal[1:-1, 1:] - gravity_coef * (elev[1:-1, 1:] - elev[1:-1, :-1])
    )
    merid_new = mask_v[1:, 1:-1] * (
        damp_v[1:, 1:-1] * merid[1:, 1:-1] - gravity_coef * (elev[1:, 1:-1] - elev[:-1, 1:-1])
    )
    flux_u = depth_u[1:-1, 1:] * zonal_new
    flux_v = depth_v[1:, 1:-1] * merid_new
    spread = flux_u[:, 1:] - flux_u[:, :-1] + (flux_v[1:, :] - flux_v[:-1, :])
    source = force_c[1:-1, 1:-1] * cosine + force_s[1:-1, 1:-1] * sine
    elev_new = mask_c[1:-1, 1:-1] * (elev[1:-1, 1:-1] - flux_coef * spread + source)
    state = jnp.stack([elev_new, zonal_new[:, :-1], merid_new[:-1, :]])
    return (state, zonal_new, merid_new)


def shards(depth_class, ocean_mask, depth_levels, drag, tide_force, forward_flow, guess):
    rows, cols = ocean_mask.shape
    tm_size = lax.axis_size("tm")
    total_rows = rows * lax.axis_size("lat")
    wide = 4

    def widen(state):
        return padded_2(state, (("lat", 1), ("lon", 2)), 4)

    classes = jnp.arange(DCLASS, dtype=jnp.int32)
    depth = jnp.sum(
        jnp.where(
            depth_class[None] == classes[:, None, None],
            depth_levels[:, None, None],
            jnp.float32(0.0),
        ),
        axis=0,
    )
    row_index = lax.axis_index("lat") * rows + jnp.arange(rows, dtype=jnp.int32)
    polar = (row_index == 0) | (row_index == total_rows - 1)
    mask = jnp.where(polar[:, None], 0, ocean_mask).astype(jnp.float32)
    stacked = jnp.stack([depth, mask, drag, tide_force[0], tide_force[1]])
    padded = padded_2(stacked, (("lat", 1), ("lon", 2)), wide + 1)
    center = padded[:, 1:-1, 1:-1]
    west_side = padded[:, 1:-1, :-2]
    south_side = padded[:, :-2, 1:-1]
    depth_u = 0.5 * (center[0] + west_side[0])
    mask_u = center[1] * west_side[1]
    damp_u = 1.0 - (center[2] + west_side[2]) / (center[0] + west_side[0])
    depth_v = 0.5 * (center[0] + south_side[0])
    mask_v = center[1] * south_side[1]
    damp_v = 1.0 - (center[2] + south_side[2]) / (center[0] + south_side[0])
    faces = (depth_u, depth_v, mask_u, mask_v, damp_u, damp_v, center[1], center[3], center[4])
    weight = mask / depth
    gain = jnp.stack(
        [
            mask,
            trim(mask_u, wide) * trim(damp_u, wide) ** STEPS,
            trim(mask_v, wide) * trim(damp_v, wide) ** STEPS,
        ]
    )
    cycle = jnp.float32(tm_size * STEPS)
    slice_index = lax.axis_index("tm")
    bound = guess[0]
    total = jnp.zeros((rows, cols), jnp.float32)
    for sweep in range(SWEEPS):
        want = sweep == SWEEPS - 1

        def block(number, carry):
            state, term = carry
            extended = widen(state)
            for sub in range(wide):
                count = slice_index * STEPS + number * wide + sub + 1
                angle = jnp.float32(2.0 * math.pi) * count.astype(jnp.float32) / cycle
                cosine, sine = (jnp.cos(angle), jnp.sin(angle))
                margin = wide - sub
                extended, zonal_new, merid_new = advance(
                    extended, margin, faces, wide, cosine, sine
                )
                if want:
                    lead = margin - 1
                    flow_u = forward_flow[0] * cosine + forward_flow[1] * sine
                    flow_v = forward_flow[2] * cosine + forward_flow[3] * sine
                    u_mid = 0.5 * (
                        zonal_new[lead : lead + rows, lead : lead + cols]
                        + zonal_new[lead : lead + rows, lead + 1 : lead + 1 + cols]
                    )
                    v_mid = 0.5 * (
                        merid_new[lead : lead + rows, lead : lead + cols]
                        + merid_new[lead + 1 : lead + 1 + rows, lead : lead + cols]
                    )
                    term = term + weight * (flow_u * u_mid + flow_v * v_mid)
            return (extended, term)

        zeros = jnp.zeros((rows, cols), jnp.float32)
        end, term = lax.fori_loop(0, STEPS // wide, block, (bound, zeros))
        if want:
            total = term
        arrived = shifted(end, "tm", 1)
        jump = arrived - bound

        def combine(earlier, later):
            return (later[0] * earlier[0], later[0] * earlier[1] + later[1])

        identity = (jnp.ones_like(gain), jnp.zeros_like(gain))
        prefix = carried_in((gain, gain * jump), "tm", combine, identity)
        change = jump + prefix[1]
        bound = bound + change
    summed = taken_together(total, "tm")
    drag_gradient = summed / jnp.float32(tm_size * STEPS)
    return (bound[None], drag_gradient)


def solution(mesh):
    return jax.shard_map(
        shards,
        mesh=mesh,
        in_specs=(
            P("lat", "lon"),
            P("lat", "lon"),
            P(),
            P("lat", "lon"),
            P(None, "lat", "lon"),
            P(None, "lat", "lon"),
            P("tm", None, "lat", "lon"),
        ),
        out_specs=(P("tm", None, "lat", "lon"), P("lat", "lon")),
        check_vma=False,
    )
```

profile of v0, /device:TPU:1, one launch (start us, length us, event | category | flops | bytes accessed | tf_op | source)
XLA Modules:
  0.0 723.1 jit_solution(9148923971574271451)
XLA Ops:
  11.0 4.6 collective-permute-start.8
  15.6 6.1 collective-permute-start.9
  23.5 5.1 collective-permute-start.10
  28.7 6.2 collective-permute-start.11
  34.9 20.1 %collective-permute-done.10 = f32[5,146,5]{2,1,0:T(8,128)S(1)} collective-permute-done((f32[5,146,5]{2,1,0:T(8,128)}, f32[5,146,5]{2,1,0:T(8,128)S(1)}, u32[]{:S(2)}, u32[]{:S(2)}) %collective-permute-start.10) | collective-permute-done | bytes 14632 | tf_op jit(solution)/shard_map/ppermute | solution.py:23
  55.0 4.9 collective-permute-done.11
  62.3 175.6 %while.63 = (s32[]{:T(128)}, f32[3,136,384]{2,1,0:T(8,128)S(1)}, f32[144,392]{1,0:T(8,128)S(1)}, f32[144,392]{1,0:T(8,128)S(1)}, f32[144,392]{1,0:T(8,128)S(1)},...) while((s32[]{:T(128)}, f32[3,136,384]{2,1,0:T(8,128)S(1)}, ...), condition=%wide.region_2.3_spmd, body=%wide.region_1.2_spmd.sunk | while | flops 5744496 | bytes 27339412 | solution.py:166
  62.3 6.3 collective-permute-start
  70.6 4.3 collective-permute-done.1
  75.8 6.1 collective-permute-start.2
  81.9 3.1 collective-permute-start.3
  86.8 16.6 %collective-permute-done.3 = f32[3,144,4]{2,1,0:T(8,128)} collective-permute-done((f32[3,144,4]{2,1,0:T(8,128)}, f32[3,144,4]{2,1,0:T(8,128)}, u32[]{:S(2)}, u32[]{:S(2)}) %collective-permute-start.3) | collective-permute-done | bytes 6944 | tf_op jit(solution)/shard_map/while/body/eval_jaxpr/ppermute | solution.py:23
  111.0 3.4 collective-permute-start
  114.4 2.2 collective-permute-start.1
  116.6 5.0 collective-permute-done.1
  124.4 7.2 collective-permute-start.3
  133.3 11.8 %collective-permute-done.3 = f32[3,144,4]{2,1,0:T(8,128)} collective-permute-done((f32[3,144,4]{2,1,0:T(8,128)}, f32[3,144,4]{2,1,0:T(8,128)}, u32[]{:S(2)}, u32[]{:S(2)}) %collective-permute-start.3) | collective-permute-done | bytes 6944 | tf_op jit(solution)/shard_map/while/body/eval_jaxpr/ppermute | solution.py:23
  152.8 4.0 collective-permute-start
  158.8 3.5 collective-permute-done.1
  163.1 3.9 collective-permute-start.2
  167.1 5.2 collective-permute-start.3
  172.9 6.8 collective-permute-done.2
  179.8 5.4 collective-permute-done.3
  192.8 4.2 collective-permute-start
  197.0 6.6 collective-permute-start.1
  205.3 4.4 collective-permute-start.2
  209.7 4.8 collective-permute-start.3
  215.2 12.4 %collective-permute-done.2 = f32[3,144,4]{2,1,0:T(8,128)} collective-permute-done((f32[3,144,4]{2,1,0:T(8,128)}, f32[3,144,4]{2,1,0:T(8,128)}, u32[]{:S(2)}, u32[]{:S(2)}) %collective-permute-start.2) | collective-permute-done | bytes 6944 | tf_op jit(solution)/shard_map/while/body/eval_jaxpr/ppermute | solution.py:26
  227.5 2.8 collective-permute-done.3
  237.9 4.4 collective-permute-start.12
  242.6 18.8 %collective-permute-done.12 = f32[3,136,384]{2,1,0:T(8,128)S(1)} collective-permute-done((f32[3,136,384]{2,1,0:T(8,128)S(1)}, f32[3,136,384]{2,1,0:T(8,128)S(1)}, u32[]{:S(2)}, u32[]{:S(2)}) %collective-permute-start.12) | collective-permute-done | bytes 626720 | tf_op jit(solution)/shard_map/ppermute | solution.py:34
  265.5 59.8 %all-gather.7.cloned.1.call-done = f32[24,136,384]{2,1,0:T(8,128)} async-done(((f32[3,136,384]{2,1,0:T(8,128)}), f32[24,136,384]{2,1,0:T(8,128)}) %all-gather.7.cloned.1.call-update) | async-done | bytes 5013520 | tf_op jit(solution)/shard_map/all_gather | solution.py:39
  325.3 66.6 %all-gather.9.cloned.1.call-done = f32[24,136,384]{2,1,0:T(8,128)} async-done(((f32[3,136,384]{2,1,0:T(8,128)}), f32[24,136,384]{2,1,0:T(8,128)}) %all-gather.9.cloned.1.call-update) | async-done | bytes 5013520 | tf_op jit(solution)/shard_map/all_gather | solution.py:39
  391.9 14.7 %while.64 = (s32[]{:T(128)}, f32[3,136,384]{2,1,0:T(8,128)S(1)}, s32[]{:T(128)}, f32[8,3,136,384]{3,2,1,0:T(8,128)}, f32[8,3,136,384]{3,2,1,0:T(8,128)}, /*index=5*/s32[]{:T(128)}, s32[]{:T(128)}) while((s32[]{:T(128)}, f32[3,136,384]{2,1,0:T(8,128)S(1)}, s32[]{:T(128)}, f32[8,3,136,384]{3,2,1,0:T(8,128)}, ...), condition=%wide.region_4.5_spmd.clone, body=%wide.region_3.4_spmd.clone.sunk | while | flops 626692 | bytes 2506853 | solution.py:51
  408.8 180.2 %while.65 = (s32[]{:T(128)}, f32[3,136,384]{2,1,0:T(8,128)S(1)}, f32[136,384]{1,0:T(8,128)S(1)}, f32[144,392]{1,0:T(8,128)S(1)}, f32[144,392]{1,0:T(8,128)S(1)},...) while((s32[]{:T(128)}, f32[3,136,384]{2,1,0:T(8,128)S(1)}, ...), condition=%wide.region_6.7_spmd.clone, body=%wide.region_5.6_spmd.clone.sunk | while | flops 8930161 | bytes 36322076 | solution.py:166
  408.8 2.7 collective-permute-start.4
  411.6 3.0 collective-permute-start.5
  417.6 7.7 %collective-permute-start.6 = (f32[3,144,4]{2,1,0:T(8,128)}, f32[3,144,4]{2,1,0:T(8,128)}, u32[]{:S(2)}, u32[]{:S(2)}) collective-permute-start(f32[3,144,4]{2,1,0:T(8,128)} %get-tuple-element.1455), channel_id=1, source_target_pairs={{1,0},{2,1},{3,2},{4,3},{5,4},{6,5},{7,6},{0,7},{9,8},{10,9},{11,1... | collective-permute-start | bytes 20744 | tf_op jit(solution)/shard_map/while/body/eval_jaxpr/ppermute | solution.py:26
  427.9 4.4 collective-permute-done.6
  432.3 13.4 %collective-permute-done.7 = f32[3,144,4]{2,1,0:T(8,128)} collective-permute-done((f32[3,144,4]{2,1,0:T(8,128)}, f32[3,144,4]{2,1,0:T(8,128)}, u32[]{:S(2)}, u32[]{:S(2)}) %collective-permute-start.7) | collective-permute-done | bytes 6944 | tf_op jit(solution)/shard_map/while/body/eval_jaxpr/ppermute | solution.py:23
  454.9 4.2 collective-permute-start.4
  459.2 2.9 collective-permute-start.5
  465.1 3.9 collective-permute-start.6
  468.9 5.3 collective-permute-start.7
  474.9 6.5 collective-permute-done.6
  481.4 8.7 %collective-permute-done.7 = f32[3,144,4]{2,1,0:T(8,128)} collective-permute-done((f32[3,144,4]{2,1,0:T(8,128)}, f32[3,144,4]{2,1,0:T(8,128)}, u32[]{:S(2)}, u32[]{:S(2)}) %collective-permute-start.7) | collective-permute-done | bytes 6944 | tf_op jit(solution)/shard_map/while/body/eval_jaxpr/ppermute | solution.py:23
  499.3 3.6 collective-permute-start.4
  504.9 3.5 collective-permute-done.5
  509.3 3.4 collective-permute-start.6
  512.6 5.8 collective-permute-start.7
  519.1 6.0 collective-permute-done.6
  525.1 7.9 %collective-permute-done.7 = f32[3,144,4]{2,1,0:T(8,128)} collective-permute-done((f32[3,144,4]{2,1,0:T(8,128)}, f32[3,144,4]{2,1,0:T(8,128)}, u32[]{:S(2)}, u32[]{:S(2)}) %collective-permute-start.7) | collective-permute-done | bytes 6944 | tf_op jit(solution)/shard_map/while/body/eval_jaxpr/ppermute | solution.py:23
  542.2 3.9 collective-permute-start.4
  546.1 4.6 collective-permute-start.5
  552.5 2.9 collective-permute-start.6
  555.4 6.3 collective-permute-start.7
  562.3 5.4 collective-permute-done.6
  567.7 12.1 %collective-permute-done.7 = f32[3,144,4]{2,1,0:T(8,128)} collective-permute-done((f32[3,144,4]{2,1,0:T(8,128)}, f32[3,144,4]{2,1,0:T(8,128)}, u32[]{:S(2)}, u32[]{:S(2)}) %collective-permute-start.7) | collective-permute-done | bytes 6944 | tf_op jit(solution)/shard_map/while/body/eval_jaxpr/ppermute | solution.py:23
  591.0 14.9 %collective-permute-done.13 = f32[3,136,384]{2,1,0:T(8,128)S(1)} collective-permute-done((f32[3,136,384]{2,1,0:T(8,128)S(1)}, f32[3,136,384]{2,1,0:T(8,128)S(1)}, u32[]{:S(2)}, u32[]{:S(2)}) %collective-permute-start.13) | collective-permute-done | bytes 626720 | tf_op jit(solution)/shard_map/ppermute | solution.py:34
  605.9 2.4 fusion.139
  609.6 3.9 all-to-all-start
  613.5 58.4 %all-to-all-done = f32[8,136,384]{2,1,0:T(8,128)S(1)} async-done(((f32[8,136,384]{2,1,0:T(8,128)}), f32[8,136,384]{2,1,0:T(8,128)S(1)}, u32[]{:S(2)}, u32[]{:S(2)}) %all-to-all-start) | async-done | bytes 1671200 | tf_op jit(solution)/shard_map/all_to_all | solution.py:56
  672.7 28.2 %all-gather.11.cloned.1.call-done = f32[24,136,384]{2,1,0:T(8,128)} async-done(((f32[3,136,384]{2,1,0:T(8,128)}), f32[24,136,384]{2,1,0:T(8,128)}) %all-gather.11.cloned.1.call-update) | async-done | bytes 5013520 | tf_op jit(solution)/shard_map/all_gather | solution.py:39
  700.9 14.7 %while.66 = (s32[]{:T(128)}, f32[3,136,384]{2,1,0:T(8,128)S(1)}, s32[]{:T(128)}, f32[8,3,136,384]{3,2,1,0:T(8,128)}, f32[8,3,136,384]{3,2,1,0:T(8,128)}, /*index=5*/s32[]{:T(128)}, s32[]{:T(128)}) while((s32[]{:T(128)}, f32[3,136,384]{2,1,0:T(8,128)S(1)}, s32[]{:T(128)}, f32[8,3,136,384]{3,2,1,0:T(8,128)}, ...), condition=%wide.region_8.9_spmd.clone, body=%wide.region_7.8_spmd.clone.sunk | while | flops 626692 | bytes 2506853 | solution.py:51
  (253 shorter events, 140.0 us)
Async XLA Ops:
  7.2 15.4 %copy-start.12 = (f32[136,384]{1,0:T(8,128)S(1)}, f32[136,384]{1,0:T(8,128)}, u32[]{:S(2)}) copy-start(f32[136,384]{1,0:T(8,128)} %param.18) | copy-start | bytes 626692
  7.2 15.4 %copy-start.8 = (f32[2,136,384]{2,1,0:T(8,128)S(1)}, f32[2,136,384]{2,1,0:T(8,128)}, u32[]{:S(2)}) copy-start(f32[2,136,384]{2,1,0:T(8,128)} %param.19) | copy-start | bytes 1253380
  7.2 318.1 %all-gather.7.cloned.1.call-start = ((), (), s32[]{:S(2)}) async-start(), calls=%async_computation.1 | async-start | bytes 5640192 | tf_op jit(solution)/shard_map/all_gather | solution.py:39
  8.4 253.0 %copy-start.4 = (f32[1,136,384]{2,1,0:T(8,128)}, f32[1,136,384]{2,1,0:T(8,128)S(1)}, u32[]{:S(2)}) copy-start(f32[1,136,384]{2,1,0:T(8,128)S(1)} %convert_bitcast_fusion) | copy-start | bytes 626692
  10.1 49.8 %copy-start.7 = (f32[136,384]{1,0:T(8,128)}, f32[136,384]{1,0:T(8,128)S(1)}, u32[]{:S(2)}) copy-start(f32[136,384]{1,0:T(8,128)S(1)} %select_reduce_fusion) | copy-start | bytes 626692
  10.1 24.7 %copy-start.5 = (f32[1,3,136,384]{3,2,1,0:T(8,128)S(1)}, f32[1,3,136,384]{3,2,1,0:T(8,128)}, u32[]{:S(2)}) copy-start(f32[1,3,136,384]{3,2,1,0:T(8,128)} %param.21) | copy-start | bytes 1880068
  11.0 10.7 %collective-permute-start.8 = (f32[5,5,384]{2,1,0:T(8,128)S(1)}, f32[5,5,384]{2,1,0:T(8,128)S(1)}, u32[]{:S(2)}, u32[]{:S(2)}) collective-permute-start(f32[5,5,384]{2,1,0:T(8,128)S(1)} %get-tuple-element.1151), channel_id=1, source_target_pairs={{0,8},{8,16},{16,24},{24,32},{32,40},{40,48},{48,56},{56,0},{1,9},... | collective-permute-start | bytes 115208 | tf_op jit(solution)/shard_map/ppermute | solution.py:23
  15.6 7.0 collective-permute-start.9
  22.6 0.9 copy-start.13
  23.5 31.5 %collective-permute-start.10 = (f32[5,146,5]{2,1,0:T(8,128)}, f32[5,146,5]{2,1,0:T(8,128)S(1)}, u32[]{:S(2)}, u32[]{:S(2)}) collective-permute-start(f32[5,146,5]{2,1,0:T(8,128)} %get-tuple-element.1149), channel_id=1, source_target_pairs={{0,1},{1,2},{2,3},{3,4},{4,5},{5,6},{6,7},{7,0},{8,9},{9,10},{10,1... | collective-permute-start | bytes 43808 | tf_op jit(solution)/shard_map/ppermute | solution.py:23
  28.7 31.3 %collective-permute-start.11 = (f32[5,146,5]{2,1,0:T(8,128)S(1)}, f32[5,146,5]{2,1,0:T(8,128)S(1)}, u32[]{:S(2)}, u32[]{:S(2)}) collective-permute-start(f32[5,146,5]{2,1,0:T(8,128)S(1)} %get-tuple-element.1150), channel_id=1, source_target_pairs={{1,0},{2,1},{3,2},{4,3},{5,4},{6,5},{7,6},{0,7},{9,8},{10,9},{11,1... | collective-permute-start | bytes 43808 | tf_op jit(solution)/shard_map/ppermute | solution.py:26
  62.3 8.2 %collective-permute-start = (f32[3,4,384]{2,1,0:T(4,128)S(1)}, f32[3,4,384]{2,1,0:T(4,128)S(1)}, u32[]{:S(2)}, u32[]{:S(2)}) collective-permute-start(f32[3,4,384]{2,1,0:T(4,128)S(1)} %get-tuple-element.1408), channel_id=1, source_target_pairs={{8,0},{16,8},{24,16},{32,24},{40,32},{48,40},{56,48},{0,56},{9,1},... | collective-permute-start | bytes 55304 | tf_op jit(solution)/shard_map/while/body/eval_jaxpr/ppermute | solution.py:26
  68.6 6.3 collective-permute-start.1
  75.8 11.0 %collective-permute-start.2 = (f32[3,144,4]{2,1,0:T(8,128)}, f32[3,144,4]{2,1,0:T(8,128)}, u32[]{:S(2)}, u32[]{:S(2)}) collective-permute-start(f32[3,144,4]{2,1,0:T(8,128)} %get-tuple-element.1410), channel_id=1, source_target_pairs={{1,0},{2,1},{3,2},{4,3},{5,4},{6,5},{7,6},{0,7},{9,8},{10,9},{11,1... | collective-permute-start | bytes 20744 | tf_op jit(solution)/shard_map/while/body/eval_jaxpr/ppermute | solution.py:26
  81.9 21.5 %collective-permute-start.3 = (f32[3,144,4]{2,1,0:T(8,128)}, f32[3,144,4]{2,1,0:T(8,128)}, u32[]{:S(2)}, u32[]{:S(2)}) collective-permute-start(f32[3,144,4]{2,1,0:T(8,128)} %get-tuple-element.1411), channel_id=1, source_target_pairs={{0,1},{1,2},{2,3},{3,4},{4,5},{5,6},{6,7},{7,0},{8,9},{9,10},{10,1... | collective-permute-start | bytes 20744 | tf_op jit(solution)/shard_map/while/body/eval_jaxpr/ppermute | solution.py:23
  111.0 5.6 collective-permute-start
  114.4 7.1 collective-permute-start.1
  122.3 11.0 %collective-permute-start.2 = (f32[3,144,4]{2,1,0:T(8,128)}, f32[3,144,4]{2,1,0:T(8,128)}, u32[]{:S(2)}, u32[]{:S(2)}) collective-permute-start(f32[3,144,4]{2,1,0:T(8,128)} %get-tuple-element.1410), channel_id=1, source_target_pairs={{1,0},{2,1},{3,2},{4,3},{5,4},{6,5},{7,6},{0,7},{9,8},{10,9},{11,1... | collective-permute-start | bytes 20744 | tf_op jit(solution)/shard_map/while/body/eval_jaxpr/ppermute | solution.py:26
  124.4 20.8 %collective-permute-start.3 = (f32[3,144,4]{2,1,0:T(8,128)}, f32[3,144,4]{2,1,0:T(8,128)}, u32[]{:S(2)}, u32[]{:S(2)}) collective-permute-start(f32[3,144,4]{2,1,0:T(8,128)} %get-tuple-element.1411), channel_id=1, source_target_pairs={{0,1},{1,2},{2,3},{3,4},{4,5},{5,6},{6,7},{7,0},{8,9},{9,10},{10,1... | collective-permute-start | bytes 20744 | tf_op jit(solution)/shard_map/while/body/eval_jaxpr/ppermute | solution.py:23
  152.8 6.0 collective-permute-start
  156.8 5.5 collective-permute-start.1
  163.1 16.7 %collective-permute-start.2 = (f32[3,144,4]{2,1,0:T(8,128)}, f32[3,144,4]{2,1,0:T(8,128)}, u32[]{:S(2)}, u32[]{:S(2)}) collective-permute-start(f32[3,144,4]{2,1,0:T(8,128)} %get-tuple-element.1410), channel_id=1, source_target_pairs={{1,0},{2,1},{3,2},{4,3},{5,4},{6,5},{7,6},{0,7},{9,8},{10,9},{11,1... | collective-permute-start | bytes 20744 | tf_op jit(solution)/shard_map/while/body/eval_jaxpr/ppermute | solution.py:26
  167.1 18.2 %collective-permute-start.3 = (f32[3,144,4]{2,1,0:T(8,128)}, f32[3,144,4]{2,1,0:T(8,128)}, u32[]{:S(2)}, u32[]{:S(2)}) collective-permute-start(f32[3,144,4]{2,1,0:T(8,128)} %get-tuple-element.1411), channel_id=1, source_target_pairs={{0,1},{1,2},{2,3},{3,4},{4,5},{5,6},{6,7},{7,0},{8,9},{9,10},{10,1... | collective-permute-start | bytes 20744 | tf_op jit(solution)/shard_map/while/body/eval_jaxpr/ppermute | solution.py:23
  192.8 10.8 %collective-permute-start = (f32[3,4,384]{2,1,0:T(4,128)S(1)}, f32[3,4,384]{2,1,0:T(4,128)S(1)}, u32[]{:S(2)}, u32[]{:S(2)}) collective-permute-start(f32[3,4,384]{2,1,0:T(4,128)S(1)} %get-tuple-element.1408), channel_id=1, source_target_pairs={{8,0},{16,8},{24,16},{32,24},{40,32},{48,40},{56,48},{0,56},{9,1},... | collective-permute-start | bytes 55304 | tf_op jit(solution)/shard_map/while/body/eval_jaxpr/ppermute | solution.py:26
  197.0 7.5 %collective-permute-start.1 = (f32[3,4,384]{2,1,0:T(4,128)S(1)}, f32[3,4,384]{2,1,0:T(4,128)S(1)}, u32[]{:S(2)}, u32[]{:S(2)}) collective-permute-start(f32[3,4,384]{2,1,0:T(4,128)S(1)} %get-tuple-element.1409), channel_id=1, source_target_pairs={{0,8},{8,16},{16,24},{24,32},{32,40},{40,48},{48,56},{56,0},{1,9},... | collective-permute-start | bytes 55304 | tf_op jit(solution)/shard_map/while/body/eval_jaxpr/ppermute | solution.py:23
  205.3 22.2 %collective-permute-start.2 = (f32[3,144,4]{2,1,0:T(8,128)}, f32[3,144,4]{2,1,0:T(8,128)}, u32[]{:S(2)}, u32[]{:S(2)}) collective-permute-start(f32[3,144,4]{2,1,0:T(8,128)} %get-tuple-element.1410), channel_id=1, source_target_pairs={{1,0},{2,1},{3,2},{4,3},{5,4},{6,5},{7,6},{0,7},{9,8},{10,9},{11,1... | collective-permute-start | bytes 20744 | tf_op jit(solution)/shard_map/while/body/eval_jaxpr/ppermute | solution.py:26
  209.7 20.6 %collective-permute-start.3 = (f32[3,144,4]{2,1,0:T(8,128)}, f32[3,144,4]{2,1,0:T(8,128)}, u32[]{:S(2)}, u32[]{:S(2)}) collective-permute-start(f32[3,144,4]{2,1,0:T(8,128)} %get-tuple-element.1411), channel_id=1, source_target_pairs={{0,1},{1,2},{2,3},{3,4},{4,5},{5,6},{6,7},{7,0},{8,9},{9,10},{10,1... | collective-permute-start | bytes 20744 | tf_op jit(solution)/shard_map/while/body/eval_jaxpr/ppermute | solution.py:23
  237.9 23.5 %copy-start.6 = (f32[1,3,136,384]{3,2,1,0:T(8,128)S(1)}, f32[1,3,136,384]{3,2,1,0:T(8,128)}, u32[]{:S(2)}) copy-start(f32[1,3,136,384]{3,2,1,0:T(8,128)} %param.21) | copy-start | bytes 1880068
  237.9 23.5 %collective-permute-start.12 = (f32[3,136,384]{2,1,0:T(8,128)S(1)}, f32[3,136,384]{2,1,0:T(8,128)S(1)}, u32[]{:S(2)}, u32[]{:S(2)}) collective-permute-start(f32[3,136,384]{2,1,0:T(8,128)S(1)} %get-tuple-element.925), channel_id=1, source_target_pairs={{0,64},{64,128},{128,192},{192,256},{256,320},{320,384},{384,448},... | collective-permute-start | bytes 1880072 | tf_op jit(solution)/shard_map/ppermute | solution.py:34
  242.6 20.1 %copy-start.10 = (f32[1,136,384]{2,1,0:T(8,128)}, f32[1,136,384]{2,1,0:T(8,128)S(1)}, u32[]{:S(2)}) copy-start(f32[1,136,384]{2,1,0:T(8,128)S(1)} %get-tuple-element.1155) | copy-start | bytes 626692
  242.6 20.0 %copy-start.11 = (f32[1,136,384]{2,1,0:T(8,128)}, f32[1,136,384]{2,1,0:T(8,128)S(1)}, u32[]{:S(2)}) copy-start(f32[1,136,384]{2,1,0:T(8,128)S(1)} %get-tuple-element.1156) | copy-start | bytes 626692
  261.4 1.2 copy-start.9
  262.7 129.2 %all-gather.9.cloned.1.call-start = ((), (), s32[]{:S(2)}) async-start(), calls=%async_computation.2 | async-start | bytes 5640192 | tf_op jit(solution)/shard_map/all_gather | solution.py:39
  263.4 437.5 %all-gather.11.cloned.1.call-start = ((), (), s32[]{:S(2)}) async-start(), calls=%async_computation.3 | async-start | bytes 5640192 | tf_op jit(solution)/shard_map/all_gather | solution.py:39
  407.9 0.8 copy-start.1
  408.8 5.8 collective-permute-start.4
  411.6 5.2 collective-permute-start.5
  417.6 14.7 %collective-permute-start.6 = (f32[3,144,4]{2,1,0:T(8,128)}, f32[3,144,4]{2,1,0:T(8,128)}, u32[]{:S(2)}, u32[]{:S(2)}) collective-permute-start(f32[3,144,4]{2,1,0:T(8,128)} %get-tuple-element.1455), channel_id=1, source_target_pairs={{1,0},{2,1},{3,2},{4,3},{5,4},{6,5},{7,6},{0,7},{9,8},{10,9},{11,1... | collective-permute-start | bytes 20744 | tf_op jit(solution)/shard_map/while/body/eval_jaxpr/ppermute | solution.py:26
  425.4 20.4 %collective-permute-start.7 = (f32[3,144,4]{2,1,0:T(8,128)}, f32[3,144,4]{2,1,0:T(8,128)}, u32[]{:S(2)}, u32[]{:S(2)}) collective-permute-start(f32[3,144,4]{2,1,0:T(8,128)} %get-tuple-element.1456), channel_id=1, source_target_pairs={{0,1},{1,2},{2,3},{3,4},{4,5},{5,6},{6,7},{7,0},{8,9},{9,10},{10,1... | collective-permute-start | bytes 20744 | tf_op jit(solution)/shard_map/while/body/eval_jaxpr/ppermute | solution.py:23
  452.9 1.2 copy-start
  452.9 1.2 copy-start.3
  454.9 7.2 collective-permute-start.4
  459.2 5.0 collective-permute-start.5
  465.1 16.4 %collective-permute-start.6 = (f32[3,144,4]{2,1,0:T(8,128)}, f32[3,144,4]{2,1,0:T(8,128)}, u32[]{:S(2)}, u32[]{:S(2)}) collective-permute-start(f32[3,144,4]{2,1,0:T(8,128)} %get-tuple-element.1455), channel_id=1, source_target_pairs={{1,0},{2,1},{3,2},{4,3},{5,4},{6,5},{7,6},{0,7},{9,8},{10,9},{11,1... | collective-permute-start | bytes 20744 | tf_op jit(solution)/shard_map/while/body/eval_jaxpr/ppermute | solution.py:26
  468.9 21.2 %collective-permute-start.7 = (f32[3,144,4]{2,1,0:T(8,128)}, f32[3,144,4]{2,1,0:T(8,128)}, u32[]{:S(2)}, u32[]{:S(2)}) collective-permute-start(f32[3,144,4]{2,1,0:T(8,128)} %get-tuple-element.1456), channel_id=1, source_target_pairs={{0,1},{1,2},{2,3},{3,4},{4,5},{5,6},{6,7},{7,0},{8,9},{9,10},{10,1... | collective-permute-start | bytes 20744 | tf_op jit(solution)/shard_map/while/body/eval_jaxpr/ppermute | solution.py:23
  497.3 1.2 copy-start
  497.3 1.2 copy-start.3
  499.3 5.6 collective-permute-start.4
  502.9 5.5 collective-permute-start.5
  509.3 15.8 %collective-permute-start.6 = (f32[3,144,4]{2,1,0:T(8,128)}, f32[3,144,4]{2,1,0:T(8,128)}, u32[]{:S(2)}, u32[]{:S(2)}) collective-permute-start(f32[3,144,4]{2,1,0:T(8,128)} %get-tuple-element.1455), channel_id=1, source_target_pairs={{1,0},{2,1},{3,2},{4,3},{5,4},{6,5},{7,6},{0,7},{9,8},{10,9},{11,1... | collective-permute-start | bytes 20744 | tf_op jit(solution)/shard_map/while/body/eval_jaxpr/ppermute | solution.py:26
  512.6 20.4 %collective-permute-start.7 = (f32[3,144,4]{2,1,0:T(8,128)}, f32[3,144,4]{2,1,0:T(8,128)}, u32[]{:S(2)}, u32[]{:S(2)}) collective-permute-start(f32[3,144,4]{2,1,0:T(8,128)} %get-tuple-element.1456), channel_id=1, source_target_pairs={{0,1},{1,2},{2,3},{3,4},{4,5},{5,6},{6,7},{7,0},{8,9},{9,10},{10,1... | collective-permute-start | bytes 20744 | tf_op jit(solution)/shard_map/while/body/eval_jaxpr/ppermute | solution.py:23
  540.2 1.2 copy-start
  540.2 1.2 copy-start.3
  542.2 8.6 %collective-permute-start.4 = (f32[3,4,384]{2,1,0:T(4,128)S(1)}, f32[3,4,384]{2,1,0:T(4,128)S(1)}, u32[]{:S(2)}, u32[]{:S(2)}) collective-permute-start(f32[3,4,384]{2,1,0:T(4,128)S(1)} %get-tuple-element.1453), channel_id=1, source_target_pairs={{8,0},{16,8},{24,16},{32,24},{40,32},{48,40},{56,48},{0,56},{9,1},... | collective-permute-start | bytes 55304 | tf_op jit(solution)/shard_map/while/body/eval_jaxpr/ppermute | solution.py:26
  546.1 5.5 collective-permute-start.5
  552.5 15.2 %collective-permute-start.6 = (f32[3,144,4]{2,1,0:T(8,128)}, f32[3,144,4]{2,1,0:T(8,128)}, u32[]{:S(2)}, u32[]{:S(2)}) collective-permute-start(f32[3,144,4]{2,1,0:T(8,128)} %get-tuple-element.1455), channel_id=1, source_target_pairs={{1,0},{2,1},{3,2},{4,3},{5,4},{6,5},{7,6},{0,7},{9,8},{10,9},{11,1... | collective-permute-start | bytes 20744 | tf_op jit(solution)/shard_map/while/body/eval_jaxpr/ppermute | solution.py:26
  555.4 24.4 %collective-permute-start.7 = (f32[3,144,4]{2,1,0:T(8,128)}, f32[3,144,4]{2,1,0:T(8,128)}, u32[]{:S(2)}, u32[]{:S(2)}) collective-permute-start(f32[3,144,4]{2,1,0:T(8,128)} %get-tuple-element.1456), channel_id=1, source_target_pairs={{0,1},{1,2},{2,3},{3,4},{4,5},{5,6},{6,7},{7,0},{8,9},{9,10},{10,1... | collective-permute-start | bytes 20744 | tf_op jit(solution)/shard_map/while/body/eval_jaxpr/ppermute | solution.py:23
  587.1 1.2 copy-start
  587.1 1.2 copy-start.3
  589.1 16.8 %collective-permute-start.13 = (f32[3,136,384]{2,1,0:T(8,128)S(1)}, f32[3,136,384]{2,1,0:T(8,128)S(1)}, u32[]{:S(2)}, u32[]{:S(2)}) collective-permute-start(f32[3,136,384]{2,1,0:T(8,128)S(1)} %get-tuple-element.927), channel_id=1, source_target_pairs={{0,64},{64,128},{128,192},{192,256},{256,320},{320,384},{384,448},... | collective-permute-start | bytes 1880072 | tf_op jit(solution)/shard_map/ppermute | solution.py:34
  609.6 62.4 %all-to-all-start = ((f32[8,136,384]{2,1,0:T(8,128)}), f32[8,136,384]{2,1,0:T(8,128)S(1)}, u32[]{:S(2)}, u32[]{:S(2)}) async-start(f32[8,136,384]{2,1,0:T(8,128)} %broadcast_in_dim.43), calls=%async_computation | async-start | bytes 3342336 | tf_op jit(solution)/shard_map/all_to_all | solution.py:56
  700.9 14.7 %copy-start.2 = (f32[3,136,384]{2,1,0:T(8,128)S(1)}, f32[3,136,384]{2,1,0:T(8,128)}, u32[]{:S(2)}) copy-start(f32[3,136,384]{2,1,0:T(8,128)} %copy-done.1) | copy-start | bytes 1880068
Sparse Core Ops, SparseCore 0:
  262.8 62.4 all-gather.6
  327.9 63.9 all-gather.8
  608.4 92.4 all-gather.10
where the time goes:
time: 726 us; the launch traced here: 723 us
  waiting for transfers between devices  418 us (58%)
  starting transfers between devices  164 us (23%)
  other arithmetic  115 us (16%)
  between operations  14 us (2%)
    all_gather x3, waiting for transfers between devices, carried_in(): everything = jax.tree.map(lambda part: lax.all_gather(part, axis), shard)  155 us
    ppermute x18, waiting for transfers between devices, padded_2(): lax.ppermute(lax.slice_in_dim(block, block.shape[dim] - width, None, axis...  121 us
    ppermute x18, starting transfers between devices, padded_2(): lax.ppermute(lax.slice_in_dim(block, 0, width, axis=dim), axis, backward)  79 us
    ppermute x18, starting transfers between devices, padded_2(): lax.ppermute(lax.slice_in_dim(block, block.shape[dim] - width, None, axis...  74.4 us
    all_to_all x1, waiting for transfers between devices, from_everyone(): return lax.all_to_all(copies, axis, split_axis=0, concat_axis=0, tiled=True)  58.4 us
    ppermute x18, waiting for transfers between devices, padded_2(): lax.ppermute(lax.slice_in_dim(block, 0, width, axis=dim), axis, backward)  49.7 us
    ppermute x2, waiting for transfers between devices, shifted(): return lax.ppermute(value, axis, pairs)  33.7 us
    select_n x16, other arithmetic, hop(): return jax.tree.map(lambda a, b: jnp.where(reached, a, b), new, before)  29.1 us
  transfers between devices with their start and end apart: 42, of which 33 were waited for; matrix products, arithmetic and copies ran while one was open for 1% of the time, Pallas kernels for 0%

commit v1 on v0

v1 whole, which is shorter than its diff:
```python
import functools
import math

import jax
import jax.numpy as jnp
import numpy as np
from jax import lax
from jax.experimental import pallas as pl
from jax.experimental.pallas import tpu as pltpu
from jax.sharding import PartitionSpec as P

STEPS = 16
NTM = 8
ROWS = 136
COLS = 384
HALO = 32
EROWS = ROWS + 2 * HALO
ECOLS = 512
NB = EROWS // 8
CROWS = 104
CB = CROWS // 8
OROWS = 72
CHUNK = 96
VMEM = pl.BlockSpec(memory_space=pltpu.VMEM)
SMEM = pl.BlockSpec(memory_space=pltpu.SMEM)
F32 = jnp.float32


def lanes(shape):
    return lax.broadcasted_iota(jnp.int32, shape, 1)


def rows_of(shape):
    return lax.broadcasted_iota(jnp.int32, shape, 0)


def turned(value, shift, axis):
    size = value.shape[axis]
    shift = shift % size
    return value if shift == 0 else pltpu.roll(value, shift, axis)


def call(kernel, out_shapes, scratch, specs):
    outs = tuple(jax.ShapeDtypeStruct(s, F32) for s in out_shapes)
    return pl.pallas_call(
        kernel,
        out_shape=outs,
        in_specs=specs,
        out_specs=tuple(VMEM for _ in outs),
        scratch_shapes=scratch,
        compiler_params=pltpu.CompilerParams(vmem_limit_bytes=60 * 1024 * 1024),
    )


def first_kernel(where_ref, levels, cls_ref, ocean_ref, drag_ref, force_ref, guess_ref, depth_ref, mask_ref, low_ref, high_ref):
    level = [levels[i] for i in range(32)]
    first, last = (where_ref[0], where_ref[1])

    def band(b, carry):
        at = pl.ds(pl.multiple_of(b * 8, 8), 8)
        cls = cls_ref[at, :]
        row = rows_of(cls.shape) + b * 8
        vals = level
        for bit in range(5):
            odd = (cls & (1 << bit)) != 0
            vals = [jnp.where(odd, vals[2 * i + 1], vals[2 * i]) for i in range(len(vals) // 2)]
        depth_ref[at, :] = vals[0]
        polar = (row == first) | (row == last)
        mask_ref[at, :] = jnp.where(polar, 0.0, ocean_ref[at, :].astype(F32))
        return carry

    lax.fori_loop(0, ROWS // 8, band, 0)
    for out, start in ((low_ref, 0), (high_ref, ROWS - HALO)):
        at = slice(start, start + HALO)
        out[0] = depth_ref[at, :]
        out[1] = mask_ref[at, :]
        out[2] = drag_ref[at, :]
        out[3] = force_ref[0, at, :]
        out[4] = force_ref[1, at, :]
        for f in range(3):
            out[5 + f] = guess_ref[f, at, :]


def own_fields(depth_ref, mask_ref, drag_ref, force_ref, guess_ref):
    views = [depth_ref, mask_ref, drag_ref, force_ref.at[0], force_ref.at[1]]
    return views + [guess_ref.at[f] for f in range(3)]


def strip_kernel(depth_ref, mask_ref, drag_ref, force_ref, guess_ref, south_ref, north_ref, west_ref, east_ref):
    own = own_fields(depth_ref, mask_ref, drag_ref, force_ref, guess_ref)
    parts = ((0, HALO, 0), (HALO, ROWS, 1), (HALO + ROWS, HALO, 2))
    for start, size, kind in parts:
        for out, tile, base in ((west_ref, 0, 0), (east_ref, COLS - 128, 96)):
            for half in range(2):
                lane = lanes((size, 128))
                packed = None
                for j in range(4):
                    f = half * 4 + j
                    src = (south_ref.at[f], own[f], north_ref.at[f])[kind]
                    piece = turned(src[:, tile : tile + 128], j * 32 - base, 1)
                    packed = piece if j == 0 else jnp.where(lane >= j * 32, piece, packed)
                out[start : start + size, half * 128 : half * 128 + 128] = packed


def south(block, before, row):
    return jnp.where(row == 0, turned(before, 1, 0), turned(block, 1, 0))


def power16(x):
    for _ in range(4):
        x = x * x
    return x


def window(ref_rows, start, tiles):
    t, r = divmod(start % (128 * tiles), 128)
    left = turned(ref_rows(t), -r, 1)
    right = turned(ref_rows((t + 1) % tiles), -r, 1)
    return jnp.where(lanes(left.shape) < 128 - r, left, right)


def sweep_kernel(
    info_ref, wave_ref, depth_ref, mask_ref, drag_ref, force_ref, guess_ref, flow_ref, south_ref, north_ref,
    from_west, from_east, out_ref, fixed_ref, flows_ref, raw, fixed, gone,
):
    own = own_fields(depth_ref, mask_ref, drag_ref, force_ref, guess_ref)
    k, keep, cy, cx = (info_ref[0], info_ref[1], info_ref[2], info_ref[3])
    for f in range(8):
        raw[f, 0:HALO, 0:COLS] = south_ref[f]
        raw[f, HALO : HALO + ROWS, 0:COLS] = own[f][...]
        raw[f, HALO + ROWS :, 0:COLS] = north_ref[f]
        j, at = (f % 4, slice(f // 4 * 128, f // 4 * 128 + 128))
        east = turned(from_east[:, at], -j * 32, 1)
        west = turned(from_west[:, at], 96 - j * 32, 1)
        lane = lanes(east.shape)
        raw[f, :, COLS:] = jnp.where(lane < 32, east, jnp.where(lane >= 96, west, 0.0))

    row = rows_of((8, ECOLS))
    keepf = keep.astype(F32)

    def prepare(b, carry):
        at = pl.ds(pl.multiple_of(b * 8, 8), 8)
        up = pl.ds(pl.multiple_of(lax.rem(b + NB - 1, NB) * 8, 8), 8)

        def pair(f):
            x = raw[f, at, :]
            before = raw[f, up, :]
            if f == 0:
                x = jnp.where(x > 0.0, x, 1.0)
                before = jnp.where(before > 0.0, before, 1.0)
            return x, turned(x, 1, 1), south(x, before, row)

        dep, dep_w, dep_s = pair(0)
        m, m_w, m_s = pair(1)
        dr, dr_w, dr_s = pair(2)
        mu, mv = (m * m_w, m * m_s)
        mdu = mu * (1.0 - (dr + dr_w) / (dep + dep_w))
        mdv = mv * (1.0 - (dr + dr_s) / (dep + dep_s))
        fixed[0, at, :] = mdu
        fixed[1, at, :] = 0.7 * mu
        fixed[2, at, :] = 0.3 * (dep + dep_w)
        fixed[3, at, :] = mdv
        fixed[4, at, :] = 0.7 * mv
        fixed[5, at, :] = 0.3 * (dep + dep_s)
        fixed[6, at, :] = m
        fixed[7, at, :] = m * raw[3, at, :]
        fixed[8, at, :] = m * raw[4, at, :]
        fixed[9, at, :] = 0.5 * m / dep
        elev = m * raw[5, at, :]
        gone[0, at, :] = keepf * elev
        gone[1, at, :] = keepf * (power16(mdu) * raw[6, at, :])
        gone[2, at, :] = keepf * (power16(mdv) * raw[7, at, :])
        return carry

    lax.fori_loop(0, NB, prepare, 0)
    for b in range(NB):
        at = slice(b * 8, b * 8 + 8)
        raw[5, at, :] = fixed[6, at, :] * raw[5, at, :]

    def step(s, carry):
        c, z = (wave_ref[0, k * STEPS + s], wave_ref[1, k * STEPS + s])
        a = raw[5, (NB - 1) * 8 :, :]
        turned_a = turned(a, 1, 0)
        after = jnp.zeros((8, ECOLS), F32)
        for b in range(NB - 1, -1, -1):
            at = slice(b * 8, b * 8 + 8)
            if b > 0:
                a_before = raw[5, b * 8 - 8 : b * 8, :]
                turned_before = turned(a_before, 1, 0)
            else:
                a_before, turned_before = (a, turned_a)
            a_s = jnp.where(row == 0, turned_before, turned_a)
            p = fixed[0, at, :] * raw[6, at, :] - fixed[1, at, :] * (a - turned(a, 1, 1))
            q = fixed[3, at, :] * raw[7, at, :] - fixed[4, at, :] * (a - a_s)
            raw[6, at, :] = p
            raw[7, at, :] = q
            fu, fv = (fixed[2, at, :] * p, fixed[5, at, :] * q)
            turned_fv = turned(fv, -1, 0)
            n_fv = jnp.where(row == 7, after, turned_fv)
            spread = (turned(fu, -1, 1) - fu) + (n_fv - fv)
            source = fixed[7, at, :] * c + fixed[8, at, :] * z
            raw[5, at, :] = (a + source) - fixed[6, at, :] * spread
            a, turned_a, after = (a_before, turned_before, turned_fv)
        return carry

    lax.fori_loop(0, STEPS, step, 0)
    for b in range(2, NB - 2):
        at = slice(b * 8, b * 8 + 8)
        for f in range(3):
            raw[5 + f, at, :] = raw[5 + f, at, :] - gone[f, at, :]

    for y in range(2):
        for f in range(3):
            at = slice(16 + 64 * y, 16 + 64 * y + CROWS)
            for x in range(4):
                tile = window(lambda t: raw[5 + f, at, t * 128 : t * 128 + 128], 96 * x - 16, 4)
                out_ref[y * 4 + x, f * CROWS : (f + 1) * CROWS, :] = tile

    top = pl.ds(pl.multiple_of(16 + 64 * cy, 8), CROWS)
    mid = pl.ds(pl.multiple_of(64 * cy, 8), OROWS)
    for x in range(4):

        @pl.when(cx == x)
        def _(x=x):
            for f in range(10):
                fixed_ref[f] = window(lambda t: fixed[f, top, t * 128 : t * 128 + 128], 96 * x - 16, 4)
            for f in range(4):
                flows_ref[f] = window(lambda t: flow_ref[f, mid, t * 128 : t * 128 + 128], 96 * x - 16, 3)


def last_kernel(wave_ref, got_ref, fixed, flows_ref, out_ref, state, old, sums):
    row = rows_of((8, 128))

    def start(b, carry):
        at = pl.ds(pl.multiple_of(b * 8, 8), 8)
        gain = (fixed[6, at, :], power16(fixed[0, at, :]), power16(fixed[3, at, :]))
        for f in range(3):
            line = pl.ds(pl.multiple_of(f * CROWS + b * 8, 8), 8)
            now = got_ref[NTM - 1, line, :]
            for k in range(NTM):
                if k > 0:
                    now = got_ref[k - 1, line, :] + gain[f] * now
                state[k, f, at, :] = now
                old[k, f, at, :] = gain[f] * now
        return carry

    lax.fori_loop(0, CB, start, 0)
    for i in range(4):
        sums[i] = jnp.zeros((CROWS, 128), F32)

    def step(s, carry):
        cs = [wave_ref[0, k * STEPS + s] for k in range(NTM)]
        zs = [wave_ref[1, k * STEPS + s] for k in range(NTM)]
        after = [jnp.zeros((8, 128), F32)] * NTM
        for b in range(CB - 1, -1, -1):
            at = slice(b * 8, b * 8 + 8)
            mdu, mu7, hu, mdv, mv7, hv, m, f0, f1 = [fixed[i, at, :] for i in range(9)]
            inside = 2 <= b <= 11
            if inside:
                total = [sums[i, at, :] for i in range(4)]
            for k in range(NTM):
                c, z = (cs[k], zs[k])
                a = state[k, 0, at, :]
                before = state[k, 0, b * 8 - 8 : b * 8, :] if b > 0 else a
                a_s = south(a, before, row)
                p = mdu * state[k, 1, at, :] - mu7 * (a - turned(a, 1, 1))
                q = mdv * state[k, 2, at, :] - mv7 * (a - a_s)
                state[k, 1, at, :] = p
                state[k, 2, at, :] = q
                if inside:
                    total[0] = total[0] + c * p
                    total[1] = total[1] + z * p
                    total[2] = total[2] + c * q
                    total[3] = total[3] + z * q
                fu, fv = (hu * p, hv * q)
                turned_fv = turned(fv, -1, 0)
                n_fv = jnp.where(row == 7, after[k], turned_fv)
                spread = (turned(fu, -1, 1) - fu) + (n_fv - fv)
                state[k, 0, at, :] = (a + (f0 * c + f1 * z)) - m * spread
                after[k] = turned_fv
            if inside:
                for i in range(4):
                    sums[i, at, :] = total[i]
        return carry

    lax.fori_loop(0, STEPS, step, 0)

    lane = lanes((8, 128))
    for b in range(OROWS // 8):
        at = slice(16 + b * 8, 24 + b * 8)
        down = slice(24 + b * 8, 32 + b * 8)
        here = slice(b * 8, b * 8 + 8)
        grad = None
        for i in range(4):
            x = sums[i, at, :]
            if i < 2:
                mid = x + turned(x, -1, 1)
            else:
                mid = x + jnp.where(row == 7, turned(sums[i, down, :], -1, 0), turned(x, -1, 0))
            part = flows_ref[i, here, :] * mid
            grad = part if grad is None else grad + part
        grad = turned(fixed[9, at, :] * grad * (1.0 / (NTM * STEPS)), 16, 1)
        gain = (fixed[6, at, :], power16(fixed[0, at, :]), power16(fixed[3, at, :]))
        now = [state[NTM - 1, f, at, :] for f in range(3)]
        for k in range(NTM):
            if k > 0:
                now = [
                    (state[k - 1, f, at, :] - old[k - 1, f, at, :]) + gain[f] * now[f] for f in range(3)
                ]
            a, p, q = (turned(now[0], -16, 1), turned(now[1], 80, 1), turned(now[2], 48, 1))
            out_ref[k, here, 0:128] = jnp.where(lane < 96, a, p)
            out_ref[k, here, 128:256] = jnp.where(lane < 64, p, q)
            out_ref[k, here, 256:384] = jnp.where(lane < 32, q, grad)


def unpack_kernel(got_ref, state_ref, grad_ref):
    lane = lanes((8, COLS))
    for b in range(ROWS // 8):
        y = 0 if b < OROWS // 8 else 1
        at = slice(b * 8 - 64 * y, b * 8 - 64 * y + 8)
        here = slice(b * 8, b * 8 + 8)
        parts = [got_ref[y * 4 + x, at, :] for x in range(4)]
        for f in range(4):
            value = turned(parts[0], -CHUNK * f, 1)
            for x in range(1, 4):
                value = jnp.where(lane >= CHUNK * x, turned(parts[x], CHUNK * (x - f), 1), value)
            if f < 3:
                state_ref[f, here, :] = value
            else:
                grad_ref[here, :] = value


def waves():
    count = np.arange(1, NTM * STEPS + 1, dtype=np.float32)
    angle = np.float32(2.0 * math.pi) * count / np.float32(NTM * STEPS)
    return np.stack([np.cos(angle), np.sin(angle)]).astype(np.float32)


def shards(depth_class, ocean_mask, depth_levels, drag, tide_force, forward_flow, guess):
    guess = guess[0]
    lat, lat_size = (lax.axis_index("lat"), lax.axis_size("lat"))
    k = lax.axis_index("tm")
    never = jnp.int32(-1)
    ends = jnp.stack([jnp.where(lat == 0, 0, never), jnp.where(lat == lat_size - 1, ROWS - 1, never)])
    info = jnp.stack([k, jnp.where(k == NTM - 1, 0, 1), k // 4, k % 4]).astype(jnp.int32)
    wave = jnp.asarray(waves())
    block = (ROWS, COLS)
    strip = (8, HALO, COLS)
    depth, mask, low, high = call(
        first_kernel, (block, block, strip, strip), [], [SMEM, SMEM] + [VMEM] * 5
    )(ends, depth_levels, depth_class, ocean_mask, drag, tide_force, guess)
    up = [(i, i + 1) for i in range(lat_size - 1)]
    down = [(i + 1, i) for i in range(lat_size - 1)]
    from_south = lax.ppermute(high, "lat", up)
    from_north = lax.ppermute(low, "lat", down)
    fields = (depth, mask, drag, tide_force, guess)
    side = (EROWS, 256)
    west, east = call(strip_kernel, (side, side), [], [VMEM] * 7)(*fields, from_south, from_north)
    lon_size = lax.axis_size("lon")
    from_west = lax.ppermute(east, "lon", [(i, (i + 1) % lon_size) for i in range(lon_size)])
    from_east = lax.ppermute(west, "lon", [((i + 1) % lon_size, i) for i in range(lon_size)])
    big = (EROWS, ECOLS)
    sent, fixed, flows = call(
        sweep_kernel,
        ((NTM, 3 * CROWS, 128), (10, CROWS, 128), (4, OROWS, 128)),
        [pltpu.VMEM((8, *big), F32), pltpu.VMEM((10, *big), F32), pltpu.VMEM((3, *big), F32)],
        [SMEM, SMEM] + [VMEM] * 10,
    )(info, wave, *fields, forward_flow, from_south, from_north, from_west, from_east)
    got = lax.all_to_all(sent, "tm", 0, 0, tiled=True)
    (back,) = call(
        last_kernel,
        ((NTM, OROWS, COLS),),
        [
            pltpu.VMEM((NTM, 3, CROWS, 128), F32),
            pltpu.VMEM((NTM, 3, CROWS, 128), F32),
            pltpu.VMEM((4, CROWS, 128), F32),
        ],
        [SMEM] + [VMEM] * 3,
    )(wave, got, fixed, flows)
    home = lax.all_to_all(back, "tm", 0, 0, tiled=True)
    state, grad = call(unpack_kernel, ((3, *block), block), [], [VMEM])(home)
    return (state[None], grad)


def solution(mesh):
    return jax.shard_map(
        shards,
        mesh=mesh,
        in_specs=(
            P("lat", "lon"),
            P("lat", "lon"),
            P(),
            P("lat", "lon"),
            P(None, "lat", "lon"),
            P(None, "lat", "lon"),
            P("tm", None, "lat", "lon"),
        ),
        out_specs=(P("tm", None, "lat", "lon"), P("lat", "lon")),
        check_vma=False,
    )
```

time: 726 us -> 155 us (0.21)
  the two profiles are of different devices: /device:TPU:1 before, /device:TPU:16 now
where the time goes in v1:
time: 155 us
  blocking collectives  74.7 us (48%)
  Pallas kernels  40.9 us (26%)
  waiting for transfers between devices  18.2 us (12%)
  starting transfers between devices  17.4 us (11%)
    all_to_all x1, blocking collectives, shards(): got = lax.all_to_all(sent, 'tm', 0, 0, tiled=True)  44.8 us
    all_to_all x1, blocking collectives, shards(): home = lax.all_to_all(back, 'tm', 0, 0, tiled=True)  29.9 us
    pallas_call x1, Pallas kernels, shards(): call(sweep_kernel, ((NTM, 3 * CROWS, 128), (10, CROWS, 128), (4, OROWS, 1...  21.2 us
    ppermute x1, waiting for transfers between devices, shards(): lax.ppermute(east, 'lon', [(i, (i + 1) % lon_size) for i in range(lon_siz...  11.4 us
    pallas_call x1, Pallas kernels, shards(): call(last_kernel, ((NTM, OROWS, COLS),), [pltpu.VMEM((NTM, 3, CROWS, 128)...  11.3 us
    ppermute x1, starting transfers between devices, shards(): lax.ppermute(west, 'lon', [((i + 1) % lon_size, i) for i in range(lon_siz...  5.92 us
    ppermute x1, starting transfers between devices, shards(): lax.ppermute(east, 'lon', [(i, (i + 1) % lon_size) for i in range(lon_siz...  5.92 us
    ppermute x1, waiting for transfers between devices, shards(): from_south = lax.ppermute(high, 'lat', up)  3.73 us
  transfers between devices with their start and end apart: 4, of which 4 were waited for; matrix products, arithmetic and copies ran while one was open for 0% of the time, Pallas kernels for 0%

profile of v1, /device:TPU:16, one launch (start us, length us, event | category | flops | bytes accessed | tf_op | source)
XLA Modules:
  0.0 154.6 jit_solution(12993992062225709025)
XLA Ops:
  0.6 0.6 pad_add_fusion.1.where_ref
  1.2 2.9 %shard_map.95 = (f32[136,384]{1,0:T(8,128)}, f32[136,384]{1,0:T(8,128)}, f32[8,32,384]{2,1,0:T(8,128)}, f32[8,32,384]{2,1,0:T(8,128)}) custom-call(s32[2]{0:T(128)} %pad_add_fusion.1.where_ref, f32[32]{0:T(128)} %levels.1, s32[136,384]{1,0:T(8,128)} %cls_ref.1, s32[136,384]{1,0:T(8,128)} %ocean_ref.1, f32[136,384]{1,0:T(8,128)} %drag_ref.5, ...), custom_call_target="tpu_custom_call" | custom-call | tf_op jit(solution)/shard_map/pallas_call | solution.py:349
  4.2 1.9 %collective-permute-start = (f32[8,32,384]{2,1,0:T(8,128)}, f32[8,32,384]{2,1,0:T(8,128)S(1)}, u32[]{:S(2)}, u32[]{:S(2)}) collective-permute-start(f32[8,32,384]{2,1,0:T(8,128)} %get-tuple-element.15), channel_id=1, source_target_pairs={{0,8},{8,16},{16,24},{24,32},{32,40},{40,48},{48,56},{1,9},{9,17},... | collective-permute-start | bytes 1179656 | tf_op jit(solution)/shard_map/ppermute | solution.py:354
  6.1 3.6 %collective-permute-start.1 = (f32[8,32,384]{2,1,0:T(8,128)}, f32[8,32,384]{2,1,0:T(8,128)S(1)}, u32[]{:S(2)}, u32[]{:S(2)}) collective-permute-start(f32[8,32,384]{2,1,0:T(8,128)} %get-tuple-element.16), channel_id=1, source_target_pairs={{8,0},{16,8},{24,16},{32,24},{40,32},{48,40},{56,48},{9,1},{17,9},... | collective-permute-start | bytes 1179656 | tf_op jit(solution)/shard_map/ppermute | solution.py:355
  9.7 3.7 %collective-permute-done.south_ref = f32[8,32,384]{2,1,0:T(8,128)S(1)} collective-permute-done((f32[8,32,384]{2,1,0:T(8,128)}, f32[8,32,384]{2,1,0:T(8,128)S(1)}, u32[]{:S(2)}, u32[]{:S(2)}) %collective-permute-start) | collective-permute-done | bytes 393248 | tf_op jit(solution)/shard_map/ppermute | solution.py:354
  13.5 0.0 copy-start
  13.5 1.9 %collective-permute-done.1.north_ref = f32[8,32,384]{2,1,0:T(8,128)S(1)} collective-permute-done((f32[8,32,384]{2,1,0:T(8,128)}, f32[8,32,384]{2,1,0:T(8,128)S(1)}, u32[]{:S(2)}, u32[]{:S(2)}) %collective-permute-start.1) | collective-permute-done | bytes 393248 | tf_op jit(solution)/shard_map/ppermute | solution.py:355
  15.3 0.0 copy-start.1
  15.3 0.0 copy-done
  15.3 0.7 copy-done.1
  16.1 2.8 %shard_map.96 = (f32[200,256]{1,0:T(8,128)}, f32[200,256]{1,0:T(8,128)}) custom-call(f32[136,384]{1,0:T(8,128)} %get-tuple-element.13.depth_ref, f32[136,384]{1,0:T(8,128)} %get-tuple-element.14.mask_ref, f32[136,384]{1,0:T(8,128)} %drag_ref.5, f32[2,136,384]{2,1,0:T(8,128)} %force_ref.5, f32[3,136,384]{2,1,0:T(8,128)} %bitcast.9, f32[8,32,384]{2,1,0:T(8,128)} %copy-done, ...), custom_call_target="tpu_custom_call" | custom-call | tf_op jit(solution)/shard_map/pallas_call | solution.py:358
  18.9 5.9 %collective-permute-start.2 = (f32[200,256]{1,0:T(8,128)}, f32[200,256]{1,0:T(8,128)S(1)}, u32[]{:S(2)}, u32[]{:S(2)}) collective-permute-start(f32[200,256]{1,0:T(8,128)} %get-tuple-element.17), channel_id=1, source_target_pairs={{0,1},{1,2},{2,3},{3,4},{4,5},{5,6},{6,7},{7,0},{8,9},{9,10},{10,1... | collective-permute-start | bytes 614408 | tf_op jit(solution)/shard_map/ppermute | solution.py:360
  24.8 5.9 %collective-permute-start.3 = (f32[200,256]{1,0:T(8,128)}, f32[200,256]{1,0:T(8,128)S(1)}, u32[]{:S(2)}, u32[]{:S(2)}) collective-permute-start(f32[200,256]{1,0:T(8,128)} %get-tuple-element.18), channel_id=1, source_target_pairs={{1,0},{2,1},{3,2},{4,3},{5,4},{6,5},{7,6},{0,7},{9,8},{10,9},{11,1... | collective-permute-start | bytes 614408 | tf_op jit(solution)/shard_map/ppermute | solution.py:361
  30.7 0.6 pad_add_fusion.info_ref
  31.3 11.4 %collective-permute-done.2.from_west = f32[200,256]{1,0:T(8,128)S(1)} collective-permute-done((f32[200,256]{1,0:T(8,128)}, f32[200,256]{1,0:T(8,128)S(1)}, u32[]{:S(2)}, u32[]{:S(2)}) %collective-permute-start.2) | collective-permute-done | bytes 204832 | tf_op jit(solution)/shard_map/ppermute | solution.py:360
  42.7 0.0 copy-start.2
  42.7 1.3 collective-permute-done.3.from_east
  44.0 0.0 copy-done.2
  44.0 0.0 copy-start.3
  44.0 0.7 copy-done.3
  44.7 21.2 %shard_map.97 = (f32[8,312,128]{2,1,0:T(8,128)}, f32[10,104,128]{2,1,0:T(8,128)}, f32[4,72,128]{2,1,0:T(8,128)}) custom-call(s32[4]{0:T(128)} %pad_add_fusion.info_ref, f32[2,128]{1,0:T(2,128)} %constant.44.clone.wave_ref, f32[136,384]{1,0:T(8,128)} %get-tuple-element.13.depth_ref, f32[136,384]{1,0:T(8,128)} %get-tuple-element.14.mask_ref, ...), custom_call_target="tpu_custom_call" | custom-call | tf_op jit(solution)/shard_map/pallas_call | solution.py:363
  65.9 44.8 %all_to_all.10.got_ref = f32[8,312,128]{2,1,0:T(8,128)} all-to-all(f32[8,312,128]{2,1,0:T(8,128)} %get-tuple-element.19), channel_id=1, replica_groups=mesh['tm'=8,'lat'=8,'lon'=8] {'tm'}, dimensions={0} | all-to-all | bytes 2555904 | tf_op jit(solution)/shard_map/all_to_all | solution.py:369
  110.7 11.3 %shard_map.98 = f32[8,72,384]{2,1,0:T(8,128)} custom-call(f32[2,128]{1,0:T(2,128)} %constant.44.clone.wave_ref, f32[8,312,128]{2,1,0:T(8,128)} %all_to_all.10.got_ref, f32[10,104,128]{2,1,0:T(8,128)} %get-tuple-element.20.fixed, f32[4,72,128]{2,1,0:T(8,128)} %get-tuple-element.21.flows_ref), custom_call_target="tpu_custom_call" | custom-call | tf_op jit(solution)/shard_map/pallas_call | solution.py:370
  122.0 29.9 %all_to_all.11.got_ref = f32[8,72,384]{2,1,0:T(8,128)} all-to-all(f32[8,72,384]{2,1,0:T(8,128)} %shard_map.98), channel_id=1, replica_groups=mesh['tm'=8,'lat'=8,'lon'=8] {'tm'}, dimensions={0} | all-to-all | bytes 1769472 | tf_op jit(solution)/shard_map/all_to_all | solution.py:380
  152.0 2.6 %shard_map.99 = (f32[3,136,384]{2,1,0:T(8,128)}, f32[136,384]{1,0:T(8,128)}) custom-call(f32[8,72,384]{2,1,0:T(8,128)} %all_to_all.11.got_ref), custom_call_target="tpu_custom_call" | custom-call | tf_op jit(solution)/shard_map/pallas_call | solution.py:381
Async XLA Ops:
  4.2 9.3 %collective-permute-start = (f32[8,32,384]{2,1,0:T(8,128)}, f32[8,32,384]{2,1,0:T(8,128)S(1)}, u32[]{:S(2)}, u32[]{:S(2)}) collective-permute-start(f32[8,32,384]{2,1,0:T(8,128)} %get-tuple-element.15), channel_id=1, source_target_pairs={{0,8},{8,16},{16,24},{24,32},{32,40},{40,48},{48,56},{1,9},{9,17},... | collective-permute-start | bytes 1179656 | tf_op jit(solution)/shard_map/ppermute | solution.py:354
  6.1 9.2 %collective-permute-start.1 = (f32[8,32,384]{2,1,0:T(8,128)}, f32[8,32,384]{2,1,0:T(8,128)S(1)}, u32[]{:S(2)}, u32[]{:S(2)}) collective-permute-start(f32[8,32,384]{2,1,0:T(8,128)} %get-tuple-element.16), channel_id=1, source_target_pairs={{8,0},{16,8},{24,16},{32,24},{40,32},{48,40},{56,48},{9,1},{17,9},... | collective-permute-start | bytes 1179656 | tf_op jit(solution)/shard_map/ppermute | solution.py:355
  13.5 1.9 %copy-start = (f32[8,32,384]{2,1,0:T(8,128)}, f32[8,32,384]{2,1,0:T(8,128)S(1)}, u32[]{:S(2)}) copy-start(f32[8,32,384]{2,1,0:T(8,128)S(1)} %collective-permute-done.south_ref) | copy-start | bytes 1179652
  15.3 0.7 copy-start.1
  18.9 23.9 %collective-permute-start.2 = (f32[200,256]{1,0:T(8,128)}, f32[200,256]{1,0:T(8,128)S(1)}, u32[]{:S(2)}, u32[]{:S(2)}) collective-permute-start(f32[200,256]{1,0:T(8,128)} %get-tuple-element.17), channel_id=1, source_target_pairs={{0,1},{1,2},{2,3},{3,4},{4,5},{5,6},{6,7},{7,0},{8,9},{9,10},{10,1... | collective-permute-start | bytes 614408 | tf_op jit(solution)/shard_map/ppermute | solution.py:360
  24.8 19.2 %collective-permute-start.3 = (f32[200,256]{1,0:T(8,128)}, f32[200,256]{1,0:T(8,128)S(1)}, u32[]{:S(2)}, u32[]{:S(2)}) collective-permute-start(f32[200,256]{1,0:T(8,128)} %get-tuple-element.18), channel_id=1, source_target_pairs={{1,0},{2,1},{3,2},{4,3},{5,4},{6,5},{7,6},{0,7},{9,8},{10,9},{11,1... | collective-permute-start | bytes 614408 | tf_op jit(solution)/shard_map/ppermute | solution.py:361
  42.7 1.3 copy-start.2
  44.0 0.7 copy-start.3

commit v2 on v1

--- a/solution.py
+++ b/solution.py
@@ -40,7 +40,7 @@
     return value if shift == 0 else pltpu.roll(value, shift, axis)
 
 
-def call(kernel, out_shapes, scratch, specs):
+def call(kernel, out_shapes, scratch, specs, mib):
     outs = tuple(jax.ShapeDtypeStruct(s, F32) for s in out_shapes)
     return pl.pallas_call(
         kernel,
@@ -48,7 +48,7 @@
         in_specs=specs,
         out_specs=tuple(VMEM for _ in outs),
         scratch_shapes=scratch,
-        compiler_params=pltpu.CompilerParams(vmem_limit_bytes=60 * 1024 * 1024),
+        compiler_params=pltpu.CompilerParams(vmem_limit_bytes=mib * 1024 * 1024),
     )
 
 
@@ -121,7 +121,7 @@
 
 def sweep_kernel(
     info_ref, wave_ref, depth_ref, mask_ref, drag_ref, force_ref, guess_ref, flow_ref, south_ref, north_ref,
-    from_west, from_east, out_ref, fixed_ref, flows_ref, raw, fixed, gone,
+    from_west, from_east, out_ref, fixed_ref, flows_ref, raw, fixed, gone, flux,
 ):
     own = own_fields(depth_ref, mask_ref, drag_ref, force_ref, guess_ref)
     k, keep, cy, cx = (info_ref[0], info_ref[1], info_ref[2], info_ref[3])
@@ -156,64 +156,60 @@
         mu, mv = (m * m_w, m * m_s)
         mdu = mu * (1.0 - (dr + dr_w) / (dep + dep_w))
         mdv = mv * (1.0 - (dr + dr_s) / (dep + dep_s))
+        hu, hv = (0.3 * (dep + dep_w), 0.3 * (dep + dep_s))
         fixed[0, at, :] = mdu
-        fixed[1, at, :] = 0.7 * mu
-        fixed[2, at, :] = 0.3 * (dep + dep_w)
-        fixed[3, at, :] = mdv
-        fixed[4, at, :] = 0.7 * mv
-        fixed[5, at, :] = 0.3 * (dep + dep_s)
-        fixed[6, at, :] = m
-        fixed[7, at, :] = m * raw[3, at, :]
-        fixed[8, at, :] = m * raw[4, at, :]
+        fixed[1, at, :] = (0.7 * mu) * hu
+        fixed[2, at, :] = mdv
+        fixed[3, at, :] = (0.7 * mv) * hv
+        fixed[4, at, :] = m * raw[3, at, :]
+        fixed[5, at, :] = m * raw[4, at, :]
+        fixed[6, at, :] = hu
+        fixed[7, at, :] = hv
+        fixed[8, at, :] = m
         fixed[9, at, :] = 0.5 * m / dep
-        elev = m * raw[5, at, :]
+        elev, zonal, merid = (m * raw[5, at, :], raw[6, at, :], raw[7, at, :])
+        flux[0, at, :] = elev
+        flux[1, at, :] = hu * zonal
+        flux[2, at, :] = hv * merid
         gone[0, at, :] = keepf * elev
-        gone[1, at, :] = keepf * (power16(mdu) * raw[6, at, :])
-        gone[2, at, :] = keepf * (power16(mdv) * raw[7, at, :])
+        gone[1, at, :] = keepf * (power16(mdu) * zonal)
+        gone[2, at, :] = keepf * (power16(mdv) * merid)
         return carry
 
     lax.fori_loop(0, NB, prepare, 0)
-    for b in range(NB):
-        at = slice(b * 8, b * 8 + 8)
-        raw[5, at, :] = fixed[6, at, :] * raw[5, at, :]
-
     def step(s, carry):
         c, z = (wave_ref[0, k * STEPS + s], wave_ref[1, k * STEPS + s])
-        a = raw[5, (NB - 1) * 8 :, :]
+        a = flux[0, EROWS - 8 :, :]
         turned_a = turned(a, 1, 0)
         after = jnp.zeros((8, ECOLS), F32)
         for b in range(NB - 1, -1, -1):
             at = slice(b * 8, b * 8 + 8)
-            if b > 0:
-                a_before = raw[5, b * 8 - 8 : b * 8, :]
-                turned_before = turned(a_before, 1, 0)
-            else:
-                a_before, turned_before = (a, turned_a)
+            a_before = flux[0, b * 8 - 8 : b * 8, :] if b > 0 else a
+            turned_before = turned(a_before, 1, 0) if b > 0 else turned_a
             a_s = jnp.where(row == 0, turned_before, turned_a)
-            p = fixed[0, at, :] * raw[6, at, :] - fixed[1, at, :] * (a - turned(a, 1, 1))
-            q = fixed[3, at, :] * raw[7, at, :] - fixed[4, at, :] * (a - a_s)
-            raw[6, at, :] = p
-            raw[7, at, :] = q
-            fu, fv = (fixed[2, at, :] * p, fixed[5, at, :] * q)
-            turned_fv = turned(fv, -1, 0)
-            n_fv = jnp.where(row == 7, after, turned_fv)
-            spread = (turned(fu, -1, 1) - fu) + (n_fv - fv)
-            source = fixed[7, at, :] * c + fixed[8, at, :] * z
-            raw[5, at, :] = (a + source) - fixed[6, at, :] * spread
-            a, turned_a, after = (a_before, turned_before, turned_fv)
+            u = fixed[0, at, :] * flux[1, at, :] - fixed[1, at, :] * (a - turned(a, 1, 1))
+            v = fixed[2, at, :] * flux[2, at, :] - fixed[3, at, :] * (a - a_s)
+            flux[1, at, :] = u
+            flux[2, at, :] = v
+            turned_v = turned(v, -1, 0)
+            v_n = jnp.where(row == 7, after, turned_v)
+            source = fixed[4, at, :] * c + fixed[5, at, :] * z
+            flux[0, at, :] = (a + source) - ((turned(u, -1, 1) - u) + (v_n - v))
+            a, turned_a, after = (a_before, turned_before, turned_v)
         return carry
 
     lax.fori_loop(0, STEPS, step, 0)
     for b in range(2, NB - 2):
         at = slice(b * 8, b * 8 + 8)
-        for f in range(3):
-            raw[5 + f, at, :] = raw[5 + f, at, :] - gone[f, at, :]
+        flux[0, at, :] = flux[0, at, :] - gone[0, at, :]
+        flux[1, at, :] = flux[1, at, :] / fixed[6, at, :] - gone[1, at, :]
+        flux[2, at, :] = flux[2, at, :] / fixed[7, at, :] - gone[2, at, :]
 
     for y in range(2):
         for f in range(3):
             at = slice(16 + 64 * y, 16 + 64 * y + CROWS)
             for x in range(4):
-                tile = window(lambda t: raw[5 + f, at, t * 128 : t * 128 + 128], 96 * x - 16, 4)
+                tile = window(lambda t: flux[f, at, t * 128 : t * 128 + 128], 96 * x - 16, 4)
                 out_ref[y * 4 + x, f * CROWS : (f + 1) * CROWS, :] = tile
 
     top = pl.ds(pl.multiple_of(16 + 64 * cy, 8), CROWS)
@@ -231,64 +227,69 @@
 def last_kernel(wave_ref, got_ref, fixed, flows_ref, out_ref, state, old, sums):
     row = rows_of((8, 128))
 
+    def gains(at):
+        return (fixed[8, at, :], power16(fixed[0, at, :]), power16(fixed[2, at, :]))
+
     def start(b, carry):
         at = pl.ds(pl.multiple_of(b * 8, 8), 8)
-        gain = (fixed[6, at, :], power16(fixed[0, at, :]), power16(fixed[3, at, :]))
+        gain = gains(at)
+        scale = (None, fixed[6, at, :], fixed[7, at, :])
         for f in range(3):
             line = pl.ds(pl.multiple_of(f * CROWS + b * 8, 8), 8)
             now = got_ref[NTM - 1, line, :]
             for k in range(NTM):
                 if k > 0:
                     now = got_ref[k - 1, line, :] + gain[f] * now
-                state[k, f, at, :] = now
+                state[k, f, at, :] = now if f == 0 else scale[f] * now
                 old[k, f, at, :] = gain[f] * now
         return carry
 
     lax.fori_loop(0, CB, start, 0)
     for i in range(4):
         sums[i] = jnp.zeros((CROWS, 128), F32)
+    half = math.sqrt(0.5)
 
     def step(s, carry):
-        cs = [wave_ref[0, k * STEPS + s] for k in range(NTM)]
-        zs = [wave_ref[1, k * STEPS + s] for k in range(NTM)]
-        after = [jnp.zeros((8, 128), F32)] * NTM
+        c, z = (wave_ref[0, s], wave_ref[1, s])
         for b in range(CB - 1, -1, -1):
             at = slice(b * 8, b * 8 + 8)
-            mdu, mu7, hu, mdv, mv7, hv, m, f0, f1 = [fixed[i, at, :] for i in range(9)]
-            inside = 2 <= b <= 11
-            if inside:
-                total = [sums[i, at, :] for i in range(4)]
-            for k in range(NTM):
-                c, z = (cs[k], zs[k])
+            mdu, ku, mdv, kv, f0, f1 = [fixed[i, at, :] for i in range(6)]
+            even, odd = (f0 * c + f1 * z, f1 * c - f0 * z)
+            source = (even, half * (odd + even), odd, half * (odd - even))
+            split = ([None] * NTM, [None] * NTM)
+            for k in (0, 4, 1, 5, 2, 6, 3, 7):
                 a = state[k, 0, at, :]
-                before = state[k, 0, b * 8 - 8 : b * 8, :] if b > 0 else a
-                a_s = south(a, before, row)
-                p = mdu * state[k, 1, at, :] - mu7 * (a - turned(a, 1, 1))
-                q = mdv * state[k, 2, at, :] - mv7 * (a - a_s)
-                state[k, 1, at, :] = p
-                state[k, 2, at, :] = q
-                if inside:
-                    total[0] = total[0] + c * p
-                    total[1] = total[1] + z * p
-                    total[2] = total[2] + c * q
-                    total[3] = total[3] + z * q
-                fu, fv = (hu * p, hv * q)
-                turned_fv = turned(fv, -1, 0)
-                n_fv = jnp.where(row == 7, after[k], turned_fv)
-                spread = (turned(fu, -1, 1) - fu) + (n_fv - fv)
-                state[k, 0, at, :] = (a + (f0 * c + f1 * z)) - m * spread
-                after[k] = turned_fv
-            if inside:
-                for i in range(4):
-                    sums[i, at, :] = total[i]
+                a_s = state[k, 0, b * 8 - 1 : b * 8 + 7, :] if b > 0 else turned(a, 1, 0)
+                u = mdu * state[k, 1, at, :] - ku * (a - turned(a, 1, 1))
+                v = mdv * state[k, 2, at, :] - kv * (a - a_s)
+                state[k, 1, at, :] = u
+                state[k, 2, at, :] = v
+                v_n = state[k, 2, b * 8 + 1 : b * 8 + 9, :] if b < CB - 1 else turned(v, -1, 0)
+                forced = a + source[k] if k < 4 else a - source[k - 4]
+                state[k, 0, at, :] = forced - ((turned(u, -1, 1) - u) + (v_n - v))
+                for part, value in zip(split, (u, v)):
+                    if k < 4:
+                        part[k] = value
+                    else:
+                        part[k - 4] = part[k - 4] - value
+            if 2 <= b <= 11:
+                for i in range(2):
+                    w = split[i]
+                    x = w[0] + half * (w[1] - w[3])
+                    y = w[2] + half * (w[1] + w[3])
+                    sums[2 * i, at, :] = sums[2 * i, at, :] + (c * x - z * y)
+                    sums[2 * i + 1, at, :] = sums[2 * i + 1, at, :] + (z * x + c * y)
         return carry
 
     lax.fori_loop(0, STEPS, step, 0)
+    for b in range(2, 12):
+        at = slice(b * 8, b * 8 + 8)
+        for i in range(4):
+            sums[i, at, :] = sums[i, at, :] / fixed[6 + i // 2, at, :]
 
     lane = lanes((8, 128))
     for b in range(OROWS // 8):
         at = slice(16 + b * 8, 24 + b * 8)
-        down = slice(24 + b * 8, 32 + b * 8)
         here = slice(b * 8, b * 8 + 8)
         grad = None
         for i in range(4):
@@ -296,17 +297,21 @@
             if i < 2:
                 mid = x + turned(x, -1, 1)
             else:
-                mid = x + jnp.where(row == 7, turned(sums[i, down, :], -1, 0), turned(x, -1, 0))
+                mid = x + sums[i, 17 + b * 8 : 25 + b * 8, :]
             part = flows_ref[i, here, :] * mid
             grad = part if grad is None else grad + part
         grad = turned(fixed[9, at, :] * grad * (1.0 / (NTM * STEPS)), 16, 1)
-        gain = (fixed[6, at, :], power16(fixed[0, at, :]), power16(fixed[3, at, :]))
-        now = [state[NTM - 1, f, at, :] for f in range(3)]
+        gain = gains(at)
+        scale = (None, 1.0 / fixed[6, at, :], 1.0 / fixed[7, at, :])
+
+        def end(k, f):
+            value = state[k, f, at, :]
+            return value if f == 0 else value * scale[f]
+
+        now = [end(NTM - 1, f) for f in range(3)]
         for k in range(NTM):
             if k > 0:
-                now = [
-                    (state[k - 1, f, at, :] - old[k - 1, f, at, :]) + gain[f] * now[f] for f in range(3)
-                ]
+                now = [(end(k - 1, f) - old[k - 1, f, at, :]) + gain[f] * now[f] for f in range(3)]
             a, p, q = (turned(now[0], -16, 1), turned(now[1], 80, 1), turned(now[2], 48, 1))
             out_ref[k, here, 0:128] = jnp.where(lane < 96, a, p)
             out_ref[k, here, 128:256] = jnp.where(lane < 64, p, q)
@@ -347,7 +352,7 @@
     block = (ROWS, COLS)
     strip = (8, HALO, COLS)
     depth, mask, low, high = call(
-        first_kernel, (block, block, strip, strip), [], [SMEM, SMEM] + [VMEM] * 5
+        first_kernel, (block, block, strip, strip), [], [SMEM, SMEM] + [VMEM] * 5, 6
     )(ends, depth_levels, depth_class, ocean_mask, drag, tide_force, guess)
     up = [(i, i + 1) for i in range(lat_size - 1)]
     down = [(i + 1, i) for i in range(lat_size - 1)]
@@ -355,7 +360,7 @@
     from_north = lax.ppermute(low, "lat", down)
     fields = (depth, mask, drag, tide_force, guess)
     side = (EROWS, 256)
-    west, east = call(strip_kernel, (side, side), [], [VMEM] * 7)(*fields, from_south, from_north)
+    west, east = call(strip_kernel, (side, side), [], [VMEM] * 7, 6)(*fields, from_south, from_north)
     lon_size = lax.axis_size("lon")
     from_west = lax.ppermute(east, "lon", [(i, (i + 1) % lon_size) for i in range(lon_size)])
     from_east = lax.ppermute(west, "lon", [((i + 1) % lon_size, i) for i in range(lon_size)])
@@ -363,8 +368,9 @@
     sent, fixed, flows = call(
         sweep_kernel,
         ((NTM, 3 * CROWS, 128), (10, CROWS, 128), (4, OROWS, 128)),
-        [pltpu.VMEM((8, *big), F32), pltpu.VMEM((10, *big), F32), pltpu.VMEM((3, *big), F32)],
+        [pltpu.VMEM((8, *big), F32), pltpu.VMEM((10, *big), F32), pltpu.VMEM((3, *big), F32), pltpu.VMEM((3, *big), F32)],
         [SMEM, SMEM] + [VMEM] * 10,
+        20,
     )(info, wave, *fields, forward_flow, from_south, from_north, from_west, from_east)
     got = lax.all_to_all(sent, "tm", 0, 0, tiled=True)
     (back,) = call(
@@ -376,9 +382,10 @@
             pltpu.VMEM((4, CROWS, 128), F32),
         ],
         [SMEM] + [VMEM] * 3,
+        10,
     )(wave, got, fixed, flows)
     home = lax.all_to_all(back, "tm", 0, 0, tiled=True)
-    state, grad = call(unpack_kernel, ((3, *block), block), [], [VMEM])(home)
+    state, grad = call(unpack_kernel, ((3, *block), block), [], [VMEM], 6)(home)
     return (state[None], grad)
 
 

time: 155 us -> 146 us (0.942)
  the two profiles are of different devices: /device:TPU:16 before, /device:TPU:18 now
where the time goes in v2:
time: 146 us
  blocking collectives  72.6 us (50%)
  Pallas kernels  30.5 us (21%)
  waiting for transfers between devices  19.7 us (13%)
  starting transfers between devices  16.3 us (11%)
  local copies, waits for them, and re-layouts  5.56 us (4%)
    all_to_all x1, blocking collectives, shards(): got = lax.all_to_all(sent, 'tm', 0, 0, tiled=True)  44.5 us
    all_to_all x1, blocking collectives, shards(): home = lax.all_to_all(back, 'tm', 0, 0, tiled=True)  28.1 us
    pallas_call x1, Pallas kernels, shards(): call(sweep_kernel, ((NTM, 3 * CROWS, 128), (10, CROWS, 128), (4, OROWS, 1...  18.3 us
    pallas_call x1, Pallas kernels, shards(): call(last_kernel, ((NTM, OROWS, COLS),), [pltpu.VMEM((NTM, 3, CROWS, 128)...  8.52 us
    ppermute x1, waiting for transfers between devices, shards(): lax.ppermute(east, 'lon', [(i, (i + 1) % lon_size) for i in range(lon_siz...  7.64 us
    ppermute x1, waiting for transfers between devices, shards(): lax.ppermute(west, 'lon', [((i + 1) % lon_size, i) for i in range(lon_siz...  6.8 us
    ppermute x1, starting transfers between devices, shards(): lax.ppermute(east, 'lon', [(i, (i + 1) % lon_size) for i in range(lon_siz...  5.92 us
    unnamed x22, local copies, waits for them, and re-layouts  5.56 us
  transfers between devices with their start and end apart: 4, of which 4 were waited for; matrix products, arithmetic and copies ran while one was open for 0% of the time, Pallas kernels for 0%

profile of v2, /device:TPU:18, one launch (start us, length us, event | category | flops | bytes accessed | tf_op | source)
XLA Modules:
  0.0 145.7 jit_solution(7557713665514622446)
XLA Ops:
  0.6 0.1 pad_add_fusion.1.where_ref
  0.7 0.0 copy-start
  0.7 1.1 copy-done
  1.8 0.0 copy-start.2
  1.8 1.0 copy-done.2
  2.8 0.0 copy-start.4
  2.8 0.9 copy-done.4
  3.7 0.0 copy-start.7
  3.7 0.9 copy-done.7
  4.7 0.0 copy-start.8
  4.7 0.9 copy-done.8
  5.6 0.0 copy-start.10
  5.6 0.7 copy-done.10
  6.3 0.0 copy-start.1
  6.3 1.1 shard_map.95
  7.4 0.0 copy-start.3
  7.4 0.0 copy-start.5
  7.4 0.0 copy-start.6
  7.4 0.0 copy-start.9
  7.4 2.1 %collective-permute-start = (f32[8,32,384]{2,1,0:T(8,128)S(1)}, f32[8,32,384]{2,1,0:T(8,128)S(1)}, u32[]{:S(2)}, u32[]{:S(2)}) collective-permute-start(f32[8,32,384]{2,1,0:T(8,128)S(1)} %get-tuple-element.15), channel_id=1, source_target_pairs={{0,8},{8,16},{16,24},{24,32},{32,40},{40,48},{48,56},{1,9},{9,17},... | collective-permute-start | bytes 1179656 | tf_op jit(solution)/shard_map/ppermute | solution.py:359
  9.5 3.6 %collective-permute-start.1 = (f32[8,32,384]{2,1,0:T(8,128)S(1)}, f32[8,32,384]{2,1,0:T(8,128)S(1)}, u32[]{:S(2)}, u32[]{:S(2)}) collective-permute-start(f32[8,32,384]{2,1,0:T(8,128)S(1)} %get-tuple-element.16), channel_id=1, source_target_pairs={{8,0},{16,8},{24,16},{32,24},{40,32},{48,40},{56,48},{9,1},{17,9},... | collective-permute-start | bytes 1179656 | tf_op jit(solution)/shard_map/ppermute | solution.py:360
  13.1 3.5 %collective-permute-done.south_ref = f32[8,32,384]{2,1,0:T(8,128)S(1)} collective-permute-done((f32[8,32,384]{2,1,0:T(8,128)S(1)}, f32[8,32,384]{2,1,0:T(8,128)S(1)}, u32[]{:S(2)}, u32[]{:S(2)}) %collective-permute-start) | collective-permute-done | bytes 393248 | tf_op jit(solution)/shard_map/ppermute | solution.py:359
  16.6 1.8 %collective-permute-done.1.north_ref = f32[8,32,384]{2,1,0:T(8,128)S(1)} collective-permute-done((f32[8,32,384]{2,1,0:T(8,128)S(1)}, f32[8,32,384]{2,1,0:T(8,128)S(1)}, u32[]{:S(2)}, u32[]{:S(2)}) %collective-permute-start.1) | collective-permute-done | bytes 393248 | tf_op jit(solution)/shard_map/ppermute | solution.py:360
  18.4 0.0 copy-done.1
  18.4 1.1 shard_map.96
  19.5 5.9 %collective-permute-start.2 = (f32[200,256]{1,0:T(8,128)}, f32[200,256]{1,0:T(8,128)S(1)}, u32[]{:S(2)}, u32[]{:S(2)}) collective-permute-start(f32[200,256]{1,0:T(8,128)} %get-tuple-element.17), channel_id=1, source_target_pairs={{0,1},{1,2},{2,3},{3,4},{4,5},{5,6},{6,7},{7,0},{8,9},{9,10},{10,1... | collective-permute-start | bytes 614408 | tf_op jit(solution)/shard_map/ppermute | solution.py:365
  25.5 4.7 %collective-permute-start.3 = (f32[200,256]{1,0:T(8,128)}, f32[200,256]{1,0:T(8,128)}, u32[]{:S(2)}, u32[]{:S(2)}) collective-permute-start(f32[200,256]{1,0:T(8,128)} %get-tuple-element.18), channel_id=1, source_target_pairs={{1,0},{2,1},{3,2},{4,3},{5,4},{6,5},{7,6},{0,7},{9,8},{10,9},{11,1... | collective-permute-start | bytes 614408 | tf_op jit(solution)/shard_map/ppermute | solution.py:366
  30.2 0.1 pad_add_fusion.info_ref
  30.3 7.6 %collective-permute-done.2.from_west = f32[200,256]{1,0:T(8,128)S(1)} collective-permute-done((f32[200,256]{1,0:T(8,128)}, f32[200,256]{1,0:T(8,128)S(1)}, u32[]{:S(2)}, u32[]{:S(2)}) %collective-permute-start.2) | collective-permute-done | bytes 204832 | tf_op jit(solution)/shard_map/ppermute | solution.py:365
  37.9 6.8 %collective-permute-done.3.from_east = f32[200,256]{1,0:T(8,128)} collective-permute-done((f32[200,256]{1,0:T(8,128)}, f32[200,256]{1,0:T(8,128)}, u32[]{:S(2)}, u32[]{:S(2)}) %collective-permute-start.3) | collective-permute-done | bytes 204832 | tf_op jit(solution)/shard_map/ppermute | solution.py:366
  44.7 0.0 copy-done.3
  44.7 0.0 copy-done.5
  44.7 0.0 copy-done.6
  44.7 0.0 copy-done.9
  44.8 18.3 %shard_map.97 = (f32[8,312,128]{2,1,0:T(8,128)S(1)}, f32[10,104,128]{2,1,0:T(8,128)S(1)}, f32[4,72,128]{2,1,0:T(8,128)S(1)}) custom-call(s32[4]{0:T(128)S(1)} %pad_add_fusion.info_ref, f32[2,128]{1,0:T(2,128)S(1)} %copy-done.9, f32[136,384]{1,0:T(8,128)S(1)} %get-tuple-element.13.depth_ref, f32[136,384]{1,0:T(8,128)S(1)} %get-tuple-element.14.mask_ref, ...), custom_call_target="tpu_custom_call" | custom-call | tf_op jit(solution)/shard_map/pallas_call | solution.py:368
  63.1 44.5 %all_to_all.10.got_ref = f32[8,312,128]{2,1,0:T(8,128)S(1)} all-to-all(f32[8,312,128]{2,1,0:T(8,128)S(1)} %get-tuple-element.19), channel_id=1, replica_groups=mesh['tm'=8,'lat'=8,'lon'=8] {'tm'}, dimensions={0} | all-to-all | bytes 2555904 | tf_op jit(solution)/shard_map/all_to_all | solution.py:375
  107.6 8.5 %shard_map.98 = f32[8,72,384]{2,1,0:T(8,128)S(1)} custom-call(f32[2,128]{1,0:T(2,128)S(1)} %copy-done.9, f32[8,312,128]{2,1,0:T(8,128)S(1)} %all_to_all.10.got_ref, f32[10,104,128]{2,1,0:T(8,128)S(1)} %get-tuple-element.20.fixed, f32[4,72,128]{2,1,0:T(8,128)S(1)} %get-tuple-element.21.flows_ref), custom_call_target="tpu_custom_call" | custom-call | tf_op jit(solution)/shard_map/pallas_call | solution.py:376
  116.1 28.1 %all_to_all.11.got_ref = f32[8,72,384]{2,1,0:T(8,128)S(1)} all-to-all(f32[8,72,384]{2,1,0:T(8,128)S(1)} %shard_map.98), channel_id=1, replica_groups=mesh['tm'=8,'lat'=8,'lon'=8] {'tm'}, dimensions={0} | all-to-all | bytes 1769472 | tf_op jit(solution)/shard_map/all_to_all | solution.py:387
  144.2 1.5 %shard_map.99 = (f32[3,136,384]{2,1,0:T(8,128)}, f32[136,384]{1,0:T(8,128)}) custom-call(f32[8,72,384]{2,1,0:T(8,128)S(1)} %all_to_all.11.got_ref), custom_call_target="tpu_custom_call" | custom-call | tf_op jit(solution)/shard_map/pallas_call | solution.py:388
Async XLA Ops:
  0.7 1.1 copy-start
  1.8 1.0 copy-start.2
  2.8 0.9 copy-start.4
  3.7 0.9 copy-start.7
  4.7 0.9 copy-start.8
  5.6 0.7 copy-start.10
  6.3 12.2 %copy-start.1 = (f32[1,3,136,384]{3,2,1,0:T(8,128)S(1)}, f32[1,3,136,384]{3,2,1,0:T(8,128)}, u32[]{:S(2)}) copy-start(f32[1,3,136,384]{3,2,1,0:T(8,128)} %param.14) | copy-start | bytes 1880068
  7.4 37.4 %copy-start.3 = (f32[2,136,384]{2,1,0:T(8,128)S(1)}, f32[2,136,384]{2,1,0:T(8,128)}, u32[]{:S(2)}) copy-start(f32[2,136,384]{2,1,0:T(8,128)} %force_ref.5) | copy-start | bytes 1253380
  7.4 37.4 %copy-start.5 = (f32[136,384]{1,0:T(8,128)S(1)}, f32[136,384]{1,0:T(8,128)}, u32[]{:S(2)}) copy-start(f32[136,384]{1,0:T(8,128)} %drag_ref.5) | copy-start | bytes 626692
  7.4 37.4 %copy-start.6 = (f32[4,136,384]{2,1,0:T(8,128)S(1)}, f32[4,136,384]{2,1,0:T(8,128)}, u32[]{:S(2)}) copy-start(f32[4,136,384]{2,1,0:T(8,128)} %flow_ref.1) | copy-start | bytes 2506756
  7.4 37.3 %copy-start.9 = (f32[2,128]{1,0:T(2,128)S(1)}, f32[2,128]{1,0:T(2,128)}, u32[]{:S(2)}) copy-start(f32[2,128]{1,0:T(2,128)} %constant.44.clone.wave_ref) | copy-start | bytes 3076
  7.4 9.2 %collective-permute-start = (f32[8,32,384]{2,1,0:T(8,128)S(1)}, f32[8,32,384]{2,1,0:T(8,128)S(1)}, u32[]{:S(2)}, u32[]{:S(2)}) collective-permute-start(f32[8,32,384]{2,1,0:T(8,128)S(1)} %get-tuple-element.15), channel_id=1, source_target_pairs={{0,8},{8,16},{16,24},{24,32},{32,40},{40,48},{48,56},{1,9},{9,17},... | collective-permute-start | bytes 1179656 | tf_op jit(solution)/shard_map/ppermute | solution.py:359
  9.5 8.9 %collective-permute-start.1 = (f32[8,32,384]{2,1,0:T(8,128)S(1)}, f32[8,32,384]{2,1,0:T(8,128)S(1)}, u32[]{:S(2)}, u32[]{:S(2)}) collective-permute-start(f32[8,32,384]{2,1,0:T(8,128)S(1)} %get-tuple-element.16), channel_id=1, source_target_pairs={{8,0},{16,8},{24,16},{32,24},{40,32},{48,40},{56,48},{9,1},{17,9},... | collective-permute-start | bytes 1179656 | tf_op jit(solution)/shard_map/ppermute | solution.py:360
  19.5 18.4 %collective-permute-start.2 = (f32[200,256]{1,0:T(8,128)}, f32[200,256]{1,0:T(8,128)S(1)}, u32[]{:S(2)}, u32[]{:S(2)}) collective-permute-start(f32[200,256]{1,0:T(8,128)} %get-tuple-element.17), channel_id=1, source_target_pairs={{0,1},{1,2},{2,3},{3,4},{4,5},{5,6},{6,7},{7,0},{8,9},{9,10},{10,1... | collective-permute-start | bytes 614408 | tf_op jit(solution)/shard_map/ppermute | solution.py:365
  25.5 19.3 %collective-permute-start.3 = (f32[200,256]{1,0:T(8,128)}, f32[200,256]{1,0:T(8,128)}, u32[]{:S(2)}, u32[]{:S(2)}) collective-permute-start(f32[200,256]{1,0:T(8,128)} %get-tuple-element.18), channel_id=1, source_target_pairs={{1,0},{2,1},{3,2},{4,3},{5,4},{6,5},{7,6},{0,7},{9,8},{10,9},{11,1... | collective-permute-start | bytes 614408 | tf_op jit(solution)/shard_map/ppermute | solution.py:366

commit v3 on v2

--- a/solution.py
+++ b/solution.py
@@ -15,7 +15,6 @@
 COLS = 384
 HALO = 32
 EROWS = ROWS + 2 * HALO
-ECOLS = 512
 NB = EROWS // 8
 CROWS = 104
 CB = CROWS // 8
@@ -24,6 +23,7 @@
 VMEM = pl.BlockSpec(memory_space=pltpu.VMEM)
 SMEM = pl.BlockSpec(memory_space=pltpu.SMEM)
 F32 = jnp.float32
+FLOPS = 60_000_000
 
 
 def lanes(shape):
@@ -40,66 +40,68 @@
     return value if shift == 0 else pltpu.roll(value, shift, axis)
 
 
-def call(kernel, out_shapes, scratch, specs, mib):
+def call(kernel, out_shapes, scratch, specs, mib, flops=0):
     outs = tuple(jax.ShapeDtypeStruct(s, F32) for s in out_shapes)
+    cost = pl.CostEstimate(flops=flops, bytes_accessed=flops // 4, transcendentals=0) if flops else None
     return pl.pallas_call(
         kernel,
         out_shape=outs,
         in_specs=specs,
         out_specs=tuple(VMEM for _ in outs),
         scratch_shapes=scratch,
+        cost_estimate=cost,
         compiler_params=pltpu.CompilerParams(vmem_limit_bytes=mib * 1024 * 1024),
     )
 
 
-def first_kernel(where_ref, levels, cls_ref, ocean_ref, drag_ref, force_ref, guess_ref, depth_ref, mask_ref, low_ref, high_ref):
+def first_kernel(
+    lat_size, lat_ref, levels_hbm, cls_hbm, ocean_hbm, drag_hbm, force_hbm, guess_hbm,
+    ground_ref, low_ref, high_ref, west_ref, east_ref,
+    levels, cls_ref, ocean_ref, drag_ref, force_ref, guess_ref, sems,
+):
+    pairs = (
+        (levels_hbm, levels), (cls_hbm, cls_ref), (ocean_hbm, ocean_ref),
+        (drag_hbm, drag_ref), (force_hbm, force_ref), (guess_hbm, guess_ref),
+    )
+    copies = [pltpu.make_async_copy(src, dst, sems.at[i]) for i, (src, dst) in enumerate(pairs)]
+    for copy in copies:
+        copy.start()
+    for copy in copies[:3]:
+        copy.wait()
     level = [levels[i] for i in range(32)]
-    first, last = (where_ref[0], where_ref[1])
-
-    def band(b, carry):
-        at = pl.ds(pl.multiple_of(b * 8, 8), 8)
+    lat = lat_ref[0]
+    first = jnp.where(lat == 0, 0, -1)
+    last = jnp.where(lat == lat_size - 1, ROWS - 1, -1)
+    for b in range(ROWS // 8):
+        at = slice(b * 8, b * 8 + 8)
         cls = cls_ref[at, :]
         row = rows_of(cls.shape) + b * 8
         vals = level
         for bit in range(5):
             odd = (cls & (1 << bit)) != 0
             vals = [jnp.where(odd, vals[2 * i + 1], vals[2 * i]) for i in range(len(vals) // 2)]
-        depth_ref[at, :] = vals[0]
+        ground_ref[0, at, :] = vals[0]
         polar = (row == first) | (row == last)
-        mask_ref[at, :] = jnp.where(polar, 0.0, ocean_ref[at, :].astype(F32))
-        return carry
-
-    lax.fori_loop(0, ROWS // 8, band, 0)
+        ground_ref[1, at, :] = jnp.where(polar, 0.0, ocean_ref[at, :].astype(F32))
+    for copy in copies[3:]:
+        copy.wait()
+    own = own_fields(ground_ref, drag_ref, force_ref, guess_ref)
     for out, start in ((low_ref, 0), (high_ref, ROWS - HALO)):
-        at = slice(start, start + HALO)
-        out[0] = depth_ref[at, :]
-        out[1] = mask_ref[at, :]
-        out[2] = drag_ref[at, :]
-        out[3] = force_ref[0, at, :]
-        out[4] = force_ref[1, at, :]
-        for f in range(3):
-            out[5 + f] = guess_ref[f, at, :]
-
-
-def own_fields(depth_ref, mask_ref, drag_ref, force_ref, guess_ref):
-    views = [depth_ref, mask_ref, drag_ref, force_ref.at[0], force_ref.at[1]]
+        for f in range(8):
+            out[f] = own[f][start : start + HALO, :]
+    lane = lanes((ROWS, 128))
+    for out, tile, base in ((west_ref, 0, 0), (east_ref, COLS - 128, 96)):
+        for half in range(2):
+            packed = None
+            for j in range(4):
+                piece = turned(own[half * 4 + j][:, tile : tile + 128], j * 32 - base, 1)
+                packed = piece if j == 0 else jnp.where(lane >= j * 32, piece, packed)
+            out[:, half * 128 : half * 128 + 128] = packed
+
+
+def own_fields(ground_ref, drag_ref, force_ref, guess_ref):
+    views = [ground_ref.at[0], ground_ref.at[1], drag_ref, force_ref.at[0], force_ref.at[1]]
     return views + [guess_ref.at[f] for f in range(3)]
-
-
-def strip_kernel(depth_ref, mask_ref, drag_ref, force_ref, guess_ref, south_ref, north_ref, west_ref, east_ref):
-    own = own_fields(depth_ref, mask_ref, drag_ref, force_ref, guess_ref)
-    parts = ((0, HALO, 0), (HALO, ROWS, 1), (HALO + ROWS, HALO, 2))
-    for start, size, kind in parts:
-        for out, tile, base in ((west_ref, 0, 0), (east_ref, COLS - 128, 96)):
-            for half in range(2):
-                lane = lanes((size, 128))
-                packed = None
-                for j in range(4):
-                    f = half * 4 + j
-                    src = (south_ref.at[f], own[f], north_ref.at[f])[kind]
-                    piece = turned(src[:, tile : tile + 128], j * 32 - base, 1)
-                    packed = piece if j == 0 else jnp.where(lane >= j * 32, piece, packed)
-                out[start : start + size, half * 128 : half * 128 + 128] = packed
 
 
 def south(block, before, row):
@@ -112,33 +114,8 @@
     return x
 
 
-def window(ref_rows, start, tiles):
-    t, r = divmod(start % (128 * tiles), 128)
-    left = turned(ref_rows(t), -r, 1)
-    right = turned(ref_rows((t + 1) % tiles), -r, 1)
-    return jnp.where(lanes(left.shape) < 128 - r, left, right)
-
-
-def sweep_kernel(
-    info_ref, wave_ref, depth_ref, mask_ref, drag_ref, force_ref, guess_ref, flow_ref, south_ref, north_ref,
-    from_west, from_east, out_ref, fixed_ref, flows_ref, raw, fixed, gone, flux,
-):
-    own = own_fields(depth_ref, mask_ref, drag_ref, force_ref, guess_ref)
-    k, keep, cy, cx = (info_ref[0], info_ref[1], info_ref[2], info_ref[3])
-    for f in range(8):
-        raw[f, 0:HALO, 0:COLS] = south_ref[f]
-        raw[f, HALO : HALO + ROWS, 0:COLS] = own[f][...]
-        raw[f, HALO + ROWS :, 0:COLS] = north_ref[f]
-        j, at = (f % 4, slice(f // 4 * 128, f // 4 * 128 + 128))
-        east = turned(from_east[:, at], -j * 32, 1)
-        west = turned(from_west[:, at], 96 - j * 32, 1)
-        lane = lanes(east.shape)
-        raw[f, :, COLS:] = jnp.where(lane < 32, east, jnp.where(lane >= 96, west, 0.0))
-
-    row = rows_of((8, ECOLS))
-    keepf = keep.astype(F32)
-
-    def prepare(b, carry):
+def prepare(raw, fixed, gone, flux, keepf, row):
+    def band(b, carry):
         at = pl.ds(pl.multiple_of(b * 8, 8), 8)
         up = pl.ds(pl.multiple_of(lax.rem(b + NB - 1, NB) * 8, 8), 8)
 
@@ -176,12 +153,15 @@
         gone[2, at, :] = keepf * (power16(mdv) * merid)
         return carry
 
-    lax.fori_loop(0, NB, prepare, 0)
+    lax.fori_loop(0, NB, band, 0, unroll=5)
+
+
+def fine(fixed, flux, gone, wave_ref, k, row):
     def step(s, carry):
         c, z = (wave_ref[0, k * STEPS + s], wave_ref[1, k * STEPS + s])
         a = flux[0, EROWS - 8 :, :]
         turned_a = turned(a, 1, 0)
-        after = jnp.zeros((8, ECOLS), F32)
+        after = jnp.zeros(a.shape, F32)
         for b in range(NB - 1, -1, -1):
             at = slice(b * 8, b * 8 + 8)
             a_before = flux[0, b * 8 - 8 : b * 8, :] if b > 0 else a
@@ -205,11 +185,67 @@
         flux[1, at, :] = flux[1, at, :] / fixed[6, at, :] - gone[1, at, :]
         flux[2, at, :] = flux[2, at, :] / fixed[7, at, :] - gone[2, at, :]
 
+
+def interior_kernel(
+    k_ref, wave_ref, ground_ref, drag_ref, force_ref, guess_ref, south_ref, north_ref,
+    fixed, flux, raw, gone,
+):
+    own = own_fields(ground_ref, drag_ref, force_ref, guess_ref)
+    k = k_ref[0]
+    for f in range(8):
+        raw[f, 0:HALO, :] = south_ref[f]
+        raw[f, HALO : HALO + ROWS, :] = own[f][...]
+        raw[f, HALO + ROWS :, :] = north_ref[f]
+    row = rows_of((8, COLS))
+    prepare(raw, fixed, gone, flux, jnp.where(k == NTM - 1, 0.0, 1.0), row)
+    fine(fixed, flux, gone, wave_ref, k, row)
+
+
+def shifted_tiles(left, right, start):
+    return jnp.where(lanes(left.shape) < 128 - start, turned(left, -start, 1), turned(right, -start, 1))
+
+
+def chunk_tile(inner, edge, x):
+    if x == 0:
+        first = edge()
+        return jnp.where(lanes(first.shape) < 32, turned(first, -16, 1), turned(inner(0), 16, 1))
+    if x == 3:
+        first = edge()
+        return jnp.where(lanes(first.shape) >= 96, turned(first, 16, 1), turned(inner(2), -16, 1))
+    return shifted_tiles(inner(x - 1), inner(x), 96 * x - 16 - 128 * (x - 1))
+
+
+def edge_kernel(
+    k_ref, wave_ref, ground_ref, drag_ref, force_ref, guess_ref, flow_ref, south_ref, north_ref,
+    from_west, from_east, corner_south, corner_north, inner_fixed, inner,
+    out_ref, fixed_ref, flows_ref, raw, fixed, gone, flux,
+):
+    own = own_fields(ground_ref, drag_ref, force_ref, guess_ref)
+    k = k_ref[0]
+    cy, cx = (lax.shift_right_logical(k, 2), k & 3)
+    for f in range(8):
+        j, at = (f % 4, slice(f // 4 * 128, f // 4 * 128 + 128))
+        parts = (
+            (0, HALO, south_ref.at[f], corner_south[0:HALO, at], corner_south[HALO:, at]),
+            (HALO, ROWS, own[f], from_west[:, at], from_east[:, at]),
+            (HALO + ROWS, HALO, north_ref.at[f], corner_north[0:HALO, at], corner_north[HALO:, at]),
+        )
+        for start, size, mine, west, east in parts:
+            lane = lanes((size, 128))
+            low = jnp.where(lane < 32, turned(west, -j * 32, 1), turned(mine[:, 0:128], 32, 1))
+            high = jnp.where(lane >= 96, turned(east, 96 - j * 32, 1), turned(mine[:, COLS - 128 :], -32, 1))
+            raw[f, start : start + size, :] = jnp.where(lane < 64, low, high)
+    row = rows_of((8, 128))
+    prepare(raw, fixed, gone, flux, jnp.where(k == NTM - 1, 0.0, 1.0), row)
+    fine(fixed, flux, gone, wave_ref, k, row)
+
     for y in range(2):
+        at = slice(16 + 64 * y, 16 + 64 * y + CROWS)
         for f in range(3):
-            at = slice(16 + 64 * y, 16 + 64 * y + CROWS)
             for x in range(4):
-                tile = window(lambda t: flux[f, at, t * 128 : t * 128 + 128], 96 * x - 16, 4)
+                tile = chunk_tile(
+                    lambda t: inner[f, at, t * 128 : t * 128 + 128], lambda: flux[f, at, :], x
+                )
                 out_ref[y * 4 + x, f * CROWS : (f + 1) * CROWS, :] = tile
 
     top = pl.ds(pl.multiple_of(16 + 64 * cy, 8), CROWS)
@@ -219,9 +255,17 @@
         @pl.when(cx == x)
         def _(x=x):
             for f in range(10):
-                fixed_ref[f] = window(lambda t: fixed[f, top, t * 128 : t * 128 + 128], 96 * x - 16, 4)
+                fixed_ref[f] = chunk_tile(
+                    lambda t: inner_fixed[f, top, t * 128 : t * 128 + 128], lambda: fixed[f, top, :], x
+                )
             for f in range(4):
-                flows_ref[f] = window(lambda t: flow_ref[f, mid, t * 128 : t * 128 + 128], 96 * x - 16, 3)
+                view = lambda t: flow_ref[f, mid, t * 128 : t * 128 + 128]
+                if x == 0:
+                    flows_ref[f] = turned(view(0), 16, 1)
+                elif x == 3:
+                    flows_ref[f] = turned(view(2), -16, 1)
+                else:
+                    flows_ref[f] = chunk_tile(view, None, x)
 
 
 def last_kernel(wave_ref, got_ref, fixed, flows_ref, out_ref, state, old, sums):
@@ -344,34 +388,62 @@
 def shards(depth_class, ocean_mask, depth_levels, drag, tide_force, forward_flow, guess):
     guess = guess[0]
     lat, lat_size = (lax.axis_index("lat"), lax.axis_size("lat"))
-    k = lax.axis_index("tm")
-    never = jnp.int32(-1)
-    ends = jnp.stack([jnp.where(lat == 0, 0, never), jnp.where(lat == lat_size - 1, ROWS - 1, never)])
-    info = jnp.stack([k, jnp.where(k == NTM - 1, 0, 1), k // 4, k % 4]).astype(jnp.int32)
+    lat = jnp.reshape(lat, (1,)).astype(jnp.int32)
+    k = jnp.reshape(lax.axis_index("tm"), (1,)).astype(jnp.int32)
     wave = jnp.asarray(waves())
     block = (ROWS, COLS)
     strip = (8, HALO, COLS)
-    depth, mask, low, high = call(
-        first_kernel, (block, block, strip, strip), [], [SMEM, SMEM] + [VMEM] * 5, 6
-    )(ends, depth_levels, depth_class, ocean_mask, drag, tide_force, guess)
+    side = (ROWS, 256)
+    ground, low, high, west, east = call(
+        functools.partial(first_kernel, lat_size),
+        ((2, *block), strip, strip, side, side),
+        [
+            pltpu.SMEM((32,), F32),
+            pltpu.VMEM(block, jnp.int32),
+            pltpu.VMEM(block, jnp.int32),
+            pltpu.VMEM(block, F32),
+            pltpu.VMEM((2, *block), F32),
+            pltpu.VMEM((3, *block), F32),
+            pltpu.SemaphoreType.DMA((6,)),
+        ],
+        [SMEM] + [pl.BlockSpec(memory_space=pltpu.HBM)] * 6,
+        60,
+    )(lat, depth_levels, depth_class, ocean_mask, drag, tide_force, guess)
     up = [(i, i + 1) for i in range(lat_size - 1)]
     down = [(i + 1, i) for i in range(lat_size - 1)]
-    from_south = lax.ppermute(high, "lat", up)
-    from_north = lax.ppermute(low, "lat", down)
-    fields = (depth, mask, drag, tide_force, guess)
-    side = (EROWS, 256)
-    west, east = call(strip_kernel, (side, side), [], [VMEM] * 7, 6)(*fields, from_south, from_north)
     lon_size = lax.axis_size("lon")
     from_west = lax.ppermute(east, "lon", [(i, (i + 1) % lon_size) for i in range(lon_size)])
     from_east = lax.ppermute(west, "lon", [((i + 1) % lon_size, i) for i in range(lon_size)])
-    big = (EROWS, ECOLS)
+    from_south = lax.ppermute(high, "lat", up)
+    from_north = lax.ppermute(low, "lat", down)
+    fields = (ground, drag, tide_force, guess)
+    inner_fixed, inner = call(
+        interior_kernel,
+        ((10, EROWS, COLS), (3, EROWS, COLS)),
+        [pltpu.VMEM((8, EROWS, COLS), F32), pltpu.VMEM((3, EROWS, COLS), F32)],
+        [SMEM, SMEM] + [VMEM] * 6,
+        8,
+        FLOPS,
+    )(k, wave, *fields, from_south, from_north)
+    to_north = jnp.concatenate([from_west[ROWS - HALO :], from_east[ROWS - HALO :]])
+    to_south = jnp.concatenate([from_west[:HALO], from_east[:HALO]])
+    corner_south = lax.ppermute(to_north, "lat", up)
+    corner_north = lax.ppermute(to_south, "lat", down)
     sent, fixed, flows = call(
-        sweep_kernel,
+        edge_kernel,
         ((NTM, 3 * CROWS, 128), (10, CROWS, 128), (4, OROWS, 128)),
-        [pltpu.VMEM((8, *big), F32), pltpu.VMEM((10, *big), F32), pltpu.VMEM((3, *big), F32), pltpu.VMEM((3, *big), F32)],
-        [SMEM, SMEM] + [VMEM] * 10,
-        20,
-    )(info, wave, *fields, forward_flow, from_south, from_north, from_west, from_east)
+        [
+            pltpu.VMEM((8, EROWS, 128), F32),
+            pltpu.VMEM((10, EROWS, 128), F32),
+            pltpu.VMEM((3, EROWS, 128), F32),
+            pltpu.VMEM((3, EROWS, 128), F32),
+        ],
+        [SMEM, SMEM] + [VMEM] * 13,
+        8,
+    )(
+        k, wave, *fields, forward_flow, from_south, from_north, from_west, from_east,
+        corner_south, corner_north, inner_fixed, inner,
+    )
     got = lax.all_to_all(sent, "tm", 0, 0, tiled=True)
     (back,) = call(
         last_kernel,

time: 146 us -> 130 us (0.89)
  the two profiles are of different devices: /device:TPU:18 before, /device:TPU:1 now
where the time goes in v3:
time: 130 us; the launch traced here: 129 us
  blocking collectives  71.4 us (55%)
  starting transfers between devices  27.9 us (21%)
  Pallas kernels  27.1 us (21%)
    all_to_all x1, blocking collectives, shards(): got = lax.all_to_all(sent, 'tm', 0, 0, tiled=True)  44.1 us
    all_to_all x1, blocking collectives, shards(): home = lax.all_to_all(back, 'tm', 0, 0, tiled=True)  27.4 us
    pallas_call x1, Pallas kernels, shards(): call(interior_kernel, ((10, EROWS, COLS), (3, EROWS, COLS)), [pltpu.VMEM(...  8.57 us
    pallas_call x1, Pallas kernels, shards(): call(last_kernel, ((NTM, OROWS, COLS),), [pltpu.VMEM((NTM, 3, CROWS, 128)...  8.55 us
    ppermute x1, starting transfers between devices, shards(): lax.ppermute(east, 'lon', [(i, (i + 1) % lon_size) for i in range(lon_siz...  8.27 us
    pallas_call x1, Pallas kernels, shards(): call(edge_kernel, ((NTM, 3 * CROWS, 128), (10, CROWS, 128), (4, OROWS, 12...  5.63 us
    ppermute x1, starting transfers between devices, shards(): from_north = lax.ppermute(low, 'lat', down)  5.48 us
    ppermute x1, starting transfers between devices, shards(): lax.ppermute(west, 'lon', [((i + 1) % lon_size, i) for i in range(lon_siz...  4.11 us
  transfers between devices with their start and end apart: 6, of which 1 were waited for; matrix products, arithmetic and copies ran while one was open for 0% of the time, Pallas kernels for 7%

profile of v3, /device:TPU:1, one launch (start us, length us, event | category | flops | bytes accessed | tf_op | source)
XLA Modules:
  0.0 129.3 jit_solution(8663841582599467853)
XLA Ops:
  0.6 0.0 copy-start.5
  0.6 0.0 copy-start.1
  0.7 0.0 copy-start.2
  0.7 0.0 copy-start
  0.7 2.9 %shard_map.95 = (f32[2,136,384]{2,1,0:T(8,128)}, f32[8,32,384]{2,1,0:T(8,128)}, f32[8,32,384]{2,1,0:T(8,128)}, f32[136,256]{1,0:T(8,128)}, f32[136,256]{1,0:T(8,128)}) custom-call(s32[1]{0:T(128)} %bitcast.1.lat_ref, f32[32]{0:T(128)} %levels_hbm.1, s32[136,384]{1,0:T(8,128)} %cls_hbm.1, s32[136,384]{1,0:T(8,128)} %ocean_hbm.1, f32[136,384]{1,0:T(8,128)} %drag_ref.3, ...), custom_call_target="tpu_custom_call" | custom-call | tf_op jit(solution)/shard_map/pallas_call | solution.py:397
  3.6 8.3 %collective-permute-start.2 = (f32[136,256]{1,0:T(8,128)}, f32[136,256]{1,0:T(8,128)S(1)}, u32[]{:S(2)}, u32[]{:S(2)}) collective-permute-start(f32[136,256]{1,0:T(8,128)} %get-tuple-element.17), channel_id=1, source_target_pairs={{0,1},{1,2},{2,3},{3,4},{4,5},{5,6},{6,7},{7,0},{8,9},{9,10},{10,1... | collective-permute-start | bytes 417800 | tf_op jit(solution)/shard_map/ppermute | solution.py:415
  11.9 4.1 %collective-permute-start.3 = (f32[136,256]{1,0:T(8,128)}, f32[136,256]{1,0:T(8,128)S(1)}, u32[]{:S(2)}, u32[]{:S(2)}) collective-permute-start(f32[136,256]{1,0:T(8,128)} %get-tuple-element.18), channel_id=1, source_target_pairs={{1,0},{2,1},{3,2},{4,3},{5,4},{6,5},{7,6},{0,7},{9,8},{10,9},{11,1... | collective-permute-start | bytes 417800 | tf_op jit(solution)/shard_map/ppermute | solution.py:416
  16.0 4.1 %collective-permute-start = (f32[8,32,384]{2,1,0:T(8,128)}, f32[8,32,384]{2,1,0:T(8,128)S(1)}, u32[]{:S(2)}, u32[]{:S(2)}) collective-permute-start(f32[8,32,384]{2,1,0:T(8,128)} %get-tuple-element.15), channel_id=1, source_target_pairs={{0,8},{8,16},{16,24},{24,32},{32,40},{40,48},{48,56},{1,9},{9,17},... | collective-permute-start | bytes 1179656 | tf_op jit(solution)/shard_map/ppermute | solution.py:417
  20.1 5.5 %collective-permute-start.1 = (f32[8,32,384]{2,1,0:T(8,128)}, f32[8,32,384]{2,1,0:T(8,128)S(1)}, u32[]{:S(2)}, u32[]{:S(2)}) collective-permute-start(f32[8,32,384]{2,1,0:T(8,128)} %get-tuple-element.16), channel_id=1, source_target_pairs={{8,0},{16,8},{24,16},{32,24},{40,32},{48,40},{56,48},{9,1},{17,9},... | collective-permute-start | bytes 1179656 | tf_op jit(solution)/shard_map/ppermute | solution.py:418
  25.6 0.0 collective-permute-done.2.from_west
  25.6 0.9 collective-permute-done.3.from_east
  26.5 1.9 %collective-permute-start.4 = (f32[64,256]{1,0:T(8,128)S(1)}, f32[64,256]{1,0:T(8,128)S(1)}, u32[]{:S(2)}, u32[]{:S(2)}) collective-permute-start(f32[64,256]{1,0:T(8,128)S(1)} %pad_maximum_fusion), channel_id=1, source_target_pairs={{0,8},{8,16},{16,24},{24,32},{32,40},{40,48},{48,56},{1,9},{9,17},... | collective-permute-start | bytes 196616 | tf_op jit(solution)/shard_map/ppermute | solution.py:430
  28.4 4.1 %collective-permute-start.5 = (f32[64,256]{1,0:T(8,128)S(1)}, f32[64,256]{1,0:T(8,128)S(1)}, u32[]{:S(2)}, u32[]{:S(2)}) collective-permute-start(f32[64,256]{1,0:T(8,128)S(1)} %pad_maximum_fusion.1), channel_id=1, source_target_pairs={{8,0},{16,8},{24,16},{32,24},{40,32},{48,40},{56,48},{9,1},{17,9},... | collective-permute-start | bytes 196616 | tf_op jit(solution)/shard_map/ppermute | solution.py:431
  32.5 0.0 collective-permute-done.south_ref
  32.5 0.0 collective-permute-done.1.north_ref
  32.5 0.0 copy-done.5
  32.6 0.0 copy-done.1
  32.6 0.0 copy-done.2
  32.6 0.0 copy-done
  32.6 0.0 copy-start.3
  32.6 1.0 copy-done.3
  33.6 0.0 copy-start.4
  33.6 8.6 %shard_map.96 = (f32[10,200,384]{2,1,0:T(8,128)S(1)}, f32[3,200,384]{2,1,0:T(8,128)S(1)}) custom-call(s32[1]{0:T(128)} %bitcast.k_ref, f32[2,128]{1,0:T(2,128)S(1)} %copy-done.5, f32[2,136,384]{2,1,0:T(8,128)S(1)} %copy-done.3, f32[136,384]{1,0:T(8,128)S(1)} %copy-done.2, f32[2,136,384]{2,1,0:T(8,128)S(1)} %copy-done.1, f32[3,136,384]{2,1,0:T(8,128)S(1)} %bitcast.5, ...), custom_call_target="tpu_custom_call" | custom-call | flops 60000000 | bytes 15000000 | tf_op jit(solution)/shard_map/pallas_call | solution.py:420
  42.2 0.0 collective-permute-done.4.corner_south
  42.2 0.0 collective-permute-done.5.corner_north
  42.2 0.0 copy-done.4
  42.2 5.6 %shard_map.97 = (f32[8,312,128]{2,1,0:T(8,128)S(1)}, f32[10,104,128]{2,1,0:T(8,128)S(1)}, f32[4,72,128]{2,1,0:T(8,128)S(1)}) custom-call(s32[1]{0:T(128)} %bitcast.k_ref, f32[2,128]{1,0:T(2,128)S(1)} %copy-done.5, f32[2,136,384]{2,1,0:T(8,128)S(1)} %copy-done.3, f32[136,384]{1,0:T(8,128)S(1)} %copy-done.2, f32[2,136,384]{2,1,0:T(8,128)S(1)} %copy-done.1, ...), custom_call_target="tpu_custom_call" | custom-call | tf_op jit(solution)/shard_map/pallas_call | solution.py:432
  47.8 44.1 %all_to_all.10.got_ref = f32[8,312,128]{2,1,0:T(8,128)S(1)} all-to-all(f32[8,312,128]{2,1,0:T(8,128)S(1)} %get-tuple-element.21), channel_id=1, replica_groups=mesh['tm'=8,'lat'=8,'lon'=8] {'tm'}, dimensions={0} | all-to-all | bytes 2555904 | tf_op jit(solution)/shard_map/all_to_all | solution.py:447
  91.9 8.6 %shard_map.98 = f32[8,72,384]{2,1,0:T(8,128)S(1)} custom-call(f32[2,128]{1,0:T(2,128)S(1)} %copy-done.5, f32[8,312,128]{2,1,0:T(8,128)S(1)} %all_to_all.10.got_ref, f32[10,104,128]{2,1,0:T(8,128)S(1)} %get-tuple-element.22.fixed, f32[4,72,128]{2,1,0:T(8,128)S(1)} %get-tuple-element.23.flows_ref), custom_call_target="tpu_custom_call" | custom-call | tf_op jit(solution)/shard_map/pallas_call | solution.py:448
  100.5 27.4 %all_to_all.11.got_ref = f32[8,72,384]{2,1,0:T(8,128)S(1)} all-to-all(f32[8,72,384]{2,1,0:T(8,128)S(1)} %shard_map.98), channel_id=1, replica_groups=mesh['tm'=8,'lat'=8,'lon'=8] {'tm'}, dimensions={0} | all-to-all | bytes 1769472 | tf_op jit(solution)/shard_map/all_to_all | solution.py:459
  127.8 1.5 %shard_map.99 = (f32[3,136,384]{2,1,0:T(8,128)}, f32[136,384]{1,0:T(8,128)}) custom-call(f32[8,72,384]{2,1,0:T(8,128)S(1)} %all_to_all.11.got_ref), custom_call_target="tpu_custom_call" | custom-call | tf_op jit(solution)/shard_map/pallas_call | solution.py:460
  (4 shorter events, 0.0 us)
Async XLA Ops:
  0.6 31.9 %copy-start.5 = (f32[2,128]{1,0:T(2,128)S(1)}, f32[2,128]{1,0:T(2,128)}, u32[]{:S(2)}) copy-start(f32[2,128]{1,0:T(2,128)} %constant.11.clone.wave_ref) | copy-start | bytes 3076
  0.6 31.9 %copy-start.1 = (f32[2,136,384]{2,1,0:T(8,128)S(1)}, f32[2,136,384]{2,1,0:T(8,128)}, u32[]{:S(2)}) copy-start(f32[2,136,384]{2,1,0:T(8,128)} %force_ref.3) | copy-start | bytes 1253380
  0.7 31.9 %copy-start.2 = (f32[136,384]{1,0:T(8,128)S(1)}, f32[136,384]{1,0:T(8,128)}, u32[]{:S(2)}) copy-start(f32[136,384]{1,0:T(8,128)} %drag_ref.3) | copy-start | bytes 626692
  0.7 31.9 %copy-start = (f32[1,3,136,384]{3,2,1,0:T(8,128)S(1)}, f32[1,3,136,384]{3,2,1,0:T(8,128)}, u32[]{:S(2)}) copy-start(f32[1,3,136,384]{3,2,1,0:T(8,128)} %param.14) | copy-start | bytes 1880068
  3.6 22.0 %collective-permute-start.2 = (f32[136,256]{1,0:T(8,128)}, f32[136,256]{1,0:T(8,128)S(1)}, u32[]{:S(2)}, u32[]{:S(2)}) collective-permute-start(f32[136,256]{1,0:T(8,128)} %get-tuple-element.17), channel_id=1, source_target_pairs={{0,1},{1,2},{2,3},{3,4},{4,5},{5,6},{6,7},{7,0},{8,9},{9,10},{10,1... | collective-permute-start | bytes 417800 | tf_op jit(solution)/shard_map/ppermute | solution.py:415
  11.9 14.6 %collective-permute-start.3 = (f32[136,256]{1,0:T(8,128)}, f32[136,256]{1,0:T(8,128)S(1)}, u32[]{:S(2)}, u32[]{:S(2)}) collective-permute-start(f32[136,256]{1,0:T(8,128)} %get-tuple-element.18), channel_id=1, source_target_pairs={{1,0},{2,1},{3,2},{4,3},{5,4},{6,5},{7,6},{0,7},{9,8},{10,9},{11,1... | collective-permute-start | bytes 417800 | tf_op jit(solution)/shard_map/ppermute | solution.py:416
  16.0 16.5 %collective-permute-start = (f32[8,32,384]{2,1,0:T(8,128)}, f32[8,32,384]{2,1,0:T(8,128)S(1)}, u32[]{:S(2)}, u32[]{:S(2)}) collective-permute-start(f32[8,32,384]{2,1,0:T(8,128)} %get-tuple-element.15), channel_id=1, source_target_pairs={{0,8},{8,16},{16,24},{24,32},{32,40},{40,48},{48,56},{1,9},{9,17},... | collective-permute-start | bytes 1179656 | tf_op jit(solution)/shard_map/ppermute | solution.py:417
  20.1 12.5 %collective-permute-start.1 = (f32[8,32,384]{2,1,0:T(8,128)}, f32[8,32,384]{2,1,0:T(8,128)S(1)}, u32[]{:S(2)}, u32[]{:S(2)}) collective-permute-start(f32[8,32,384]{2,1,0:T(8,128)} %get-tuple-element.16), channel_id=1, source_target_pairs={{8,0},{16,8},{24,16},{32,24},{40,32},{48,40},{56,48},{9,1},{17,9},... | collective-permute-start | bytes 1179656 | tf_op jit(solution)/shard_map/ppermute | solution.py:418
  26.5 15.7 %collective-permute-start.4 = (f32[64,256]{1,0:T(8,128)S(1)}, f32[64,256]{1,0:T(8,128)S(1)}, u32[]{:S(2)}, u32[]{:S(2)}) collective-permute-start(f32[64,256]{1,0:T(8,128)S(1)} %pad_maximum_fusion), channel_id=1, source_target_pairs={{0,8},{8,16},{16,24},{24,32},{32,40},{40,48},{48,56},{1,9},{9,17},... | collective-permute-start | bytes 196616 | tf_op jit(solution)/shard_map/ppermute | solution.py:430
  28.4 13.8 %collective-permute-start.5 = (f32[64,256]{1,0:T(8,128)S(1)}, f32[64,256]{1,0:T(8,128)S(1)}, u32[]{:S(2)}, u32[]{:S(2)}) collective-permute-start(f32[64,256]{1,0:T(8,128)S(1)} %pad_maximum_fusion.1), channel_id=1, source_target_pairs={{8,0},{16,8},{24,16},{32,24},{40,32},{48,40},{56,48},{9,1},{17,9},... | collective-permute-start | bytes 196616 | tf_op jit(solution)/shard_map/ppermute | solution.py:431
  32.6 1.0 copy-start.3
  33.6 8.6 %copy-start.4 = (f32[4,136,384]{2,1,0:T(8,128)S(1)}, f32[4,136,384]{2,1,0:T(8,128)}, u32[]{:S(2)}) copy-start(f32[4,136,384]{2,1,0:T(8,128)} %flow_ref.1) | copy-start | bytes 2506756

commit v4 on v3

--- a/solution.py
+++ b/solution.py
@@ -23,7 +23,8 @@
 VMEM = pl.BlockSpec(memory_space=pltpu.VMEM)
 SMEM = pl.BlockSpec(memory_space=pltpu.SMEM)
 F32 = jnp.float32
-FLOPS = 60_000_000
+FLOPS = 30_000_000
+SPLIT = 9
 
 
 def lanes(shape):
@@ -156,7 +157,7 @@
     lax.fori_loop(0, NB, band, 0, unroll=5)
 
 
-def fine(fixed, flux, gone, wave_ref, k, row):
+def fine(fixed, flux, wave_ref, k, row, first, last):
     def step(s, carry):
         c, z = (wave_ref[0, k * STEPS + s], wave_ref[1, k * STEPS + s])
         a = flux[0, EROWS - 8 :, :]
@@ -178,7 +179,10 @@
             a, turned_a, after = (a_before, turned_before, turned_v)
         return carry
 
-    lax.fori_loop(0, STEPS, step, 0)
+    lax.fori_loop(first, last, step, 0)
+
+
+def finish(fixed, flux, gone):
     for b in range(2, NB - 2):
         at = slice(b * 8, b * 8 + 8)
         flux[0, at, :] = flux[0, at, :] - gone[0, at, :]
@@ -187,8 +191,7 @@
 
 
 def interior_kernel(
-    k_ref, wave_ref, ground_ref, drag_ref, force_ref, guess_ref, south_ref, north_ref,
-    fixed, flux, raw, gone,
+    k_ref, wave_ref, ground_ref, drag_ref, force_ref, guess_ref, south_ref, north_ref, fixed, flux, gone, raw,
 ):
     own = own_fields(ground_ref, drag_ref, force_ref, guess_ref)
     k = k_ref[0]
@@ -198,7 +201,14 @@
         raw[f, HALO + ROWS :, :] = north_ref[f]
     row = rows_of((8, COLS))
     prepare(raw, fixed, gone, flux, jnp.where(k == NTM - 1, 0.0, 1.0), row)
-    fine(fixed, flux, gone, wave_ref, k, row)
+    fine(fixed, flux, wave_ref, k, row, 0, SPLIT)
+
+
+def second_kernel(k_ref, wave_ref, fixed, before, gone, flux):
+    for f in range(3):
+        flux[f] = before[f]
+    fine(fixed, flux, wave_ref, k_ref[0], rows_of((8, COLS)), SPLIT, STEPS)
+    finish(fixed, flux, gone)
 
 
 def shifted_tiles(left, right, start):
@@ -237,7 +247,8 @@
             raw[f, start : start + size, :] = jnp.where(lane < 64, low, high)
     row = rows_of((8, 128))
     prepare(raw, fixed, gone, flux, jnp.where(k == NTM - 1, 0.0, 1.0), row)
-    fine(fixed, flux, gone, wave_ref, k, row)
+    fine(fixed, flux, wave_ref, k, row, 0, STEPS)
+    finish(fixed, flux, gone)
 
     for y in range(2):
         at = slice(16 + 64 * y, 16 + 64 * y + CROWS)
@@ -417,14 +428,19 @@
     from_south = lax.ppermute(high, "lat", up)
     from_north = lax.ppermute(low, "lat", down)
     fields = (ground, drag, tide_force, guess)
-    inner_fixed, inner = call(
+    deep = (3, EROWS, COLS)
+    inner_fixed, half, gone = call(
         interior_kernel,
-        ((10, EROWS, COLS), (3, EROWS, COLS)),
-        [pltpu.VMEM((8, EROWS, COLS), F32), pltpu.VMEM((3, EROWS, COLS), F32)],
+        ((10, EROWS, COLS), deep, deep),
+        [pltpu.VMEM((8, EROWS, COLS), F32)],
         [SMEM, SMEM] + [VMEM] * 6,
         8,
         FLOPS,
     )(k, wave, *fields, from_south, from_north)
+    from_west, from_east, half = lax.optimization_barrier((from_west, from_east, half))
+    (inner,) = call(second_kernel, (deep,), [], [SMEM, SMEM] + [VMEM] * 3, 4, FLOPS)(
+        k, wave, inner_fixed, half, gone
+    )
     to_north = jnp.concatenate([from_west[ROWS - HALO :], from_east[ROWS - HALO :]])
     to_south = jnp.concatenate([from_west[:HALO], from_east[:HALO]])
     corner_south = lax.ppermute(to_north, "lat", up)

time: 130 us -> 128 us (0.985)
  blocking collectives: 71.4 us -> 69.4 us
    ppermute x1, starting transfers between devices: 8.27 us -> 3 us  [shards(): lax.ppermute(east, 'lon', [(i, (i + 1) % lon_size) for i in range(lon_siz...]
    ppermute x1, starting transfers between devices: 4.11 us -> 8.3 us  [shards(): lax.ppermute(west, 'lon', [((i + 1) % lon_size, i) for i in range(lon_siz...]
    ppermute x1, starting transfers between devices: 1.92 us -> 4.54 us  [shards(): corner_south = lax.ppermute(to_north, 'lat', up)]
    all_to_all x1, blocking collectives: 44.1 us -> 41.9 us  [shards(): got = lax.all_to_all(sent, 'tm', 0, 0, tiled=True)]
    ppermute x1, starting transfers between devices: 4.08 us -> 1.92 us  [shards(): corner_north = lax.ppermute(to_south, 'lat', down)]
    pallas_call x1 -> x2, Pallas kernels: 8.57 us -> 9.25 us  [the longest x1 5.45 us: shards(): call(interior_kernel, ((10, EROWS, COLS), deep, deep), [pltpu.VMEM((8, ER...]
where the time goes in v4:
time: 128 us
  blocking collectives  69.4 us (54%)
  Pallas kernels  27.8 us (22%)
  starting transfers between devices  27.8 us (22%)
    all_to_all x1, blocking collectives, shards(): got = lax.all_to_all(sent, 'tm', 0, 0, tiled=True)  41.9 us
    all_to_all x1, blocking collectives, shards(): home = lax.all_to_all(back, 'tm', 0, 0, tiled=True)  27.5 us
    pallas_call x1, Pallas kernels, shards(): call(last_kernel, ((NTM, OROWS, COLS),), [pltpu.VMEM((NTM, 3, CROWS, 128)...  8.55 us
    ppermute x1, starting transfers between devices, shards(): lax.ppermute(west, 'lon', [((i + 1) % lon_size, i) for i in range(lon_siz...  8.3 us
    pallas_call x1, Pallas kernels, shards(): call(edge_kernel, ((NTM, 3 * CROWS, 128), (10, CROWS, 128), (4, OROWS, 12...  5.64 us
    ppermute x1, starting transfers between devices, shards(): from_north = lax.ppermute(low, 'lat', down)  5.48 us
    pallas_call x1, Pallas kernels, shards(): call(interior_kernel, ((10, EROWS, COLS), deep, deep), [pltpu.VMEM((8, ER...  5.45 us
    ppermute x1, starting transfers between devices, shards(): from_south = lax.ppermute(high, 'lat', up)  4.58 us
  transfers between devices with their start and end apart: 6, of which 1 were waited for; matrix products, arithmetic and copies ran while one was open for 0% of the time, Pallas kernels for 7%

profile of v4, /device:TPU:1, one launch (start us, length us, event | category | flops | bytes accessed | tf_op | source)
XLA Modules:
  0.0 128.1 jit_solution(15731294787256084964)
XLA Ops:
  0.6 0.0 copy-start.6
  0.6 0.0 copy-start.1
  0.7 0.0 copy-start.2
  0.7 0.0 copy-start
  0.7 2.9 %shard_map.95 = (f32[2,136,384]{2,1,0:T(8,128)}, f32[8,32,384]{2,1,0:T(8,128)}, f32[8,32,384]{2,1,0:T(8,128)}, f32[136,256]{1,0:T(8,128)}, f32[136,256]{1,0:T(8,128)}) custom-call(s32[1]{0:T(128)} %bitcast.1.lat_ref, f32[32]{0:T(128)} %levels_hbm.1, s32[136,384]{1,0:T(8,128)} %cls_hbm.1, s32[136,384]{1,0:T(8,128)} %ocean_hbm.1, f32[136,384]{1,0:T(8,128)} %drag_ref.3, ...), custom_call_target="tpu_custom_call" | custom-call | tf_op jit(solution)/shard_map/pallas_call | solution.py:408
  3.6 4.6 %collective-permute-start = (f32[8,32,384]{2,1,0:T(8,128)}, f32[8,32,384]{2,1,0:T(8,128)S(1)}, u32[]{:S(2)}, u32[]{:S(2)}) collective-permute-start(f32[8,32,384]{2,1,0:T(8,128)} %get-tuple-element.19), channel_id=1, source_target_pairs={{0,8},{8,16},{16,24},{24,32},{32,40},{40,48},{48,56},{1,9},{9,17},... | collective-permute-start | bytes 1179656 | tf_op jit(solution)/shard_map/ppermute | solution.py:428
  8.2 5.5 %collective-permute-start.1 = (f32[8,32,384]{2,1,0:T(8,128)}, f32[8,32,384]{2,1,0:T(8,128)S(1)}, u32[]{:S(2)}, u32[]{:S(2)}) collective-permute-start(f32[8,32,384]{2,1,0:T(8,128)} %get-tuple-element.20), channel_id=1, source_target_pairs={{8,0},{16,8},{24,16},{32,24},{40,32},{48,40},{56,48},{9,1},{17,9},... | collective-permute-start | bytes 1179656 | tf_op jit(solution)/shard_map/ppermute | solution.py:429
  13.7 3.0 %collective-permute-start.2 = (f32[136,256]{1,0:T(8,128)}, f32[136,256]{1,0:T(8,128)S(1)}, u32[]{:S(2)}, u32[]{:S(2)}) collective-permute-start(f32[136,256]{1,0:T(8,128)} %get-tuple-element.21), channel_id=1, source_target_pairs={{0,1},{1,2},{2,3},{3,4},{4,5},{5,6},{6,7},{7,0},{8,9},{9,10},{10,1... | collective-permute-start | bytes 417800 | tf_op jit(solution)/shard_map/ppermute | solution.py:426
  16.7 8.3 %collective-permute-start.3 = (f32[136,256]{1,0:T(8,128)}, f32[136,256]{1,0:T(8,128)S(1)}, u32[]{:S(2)}, u32[]{:S(2)}) collective-permute-start(f32[136,256]{1,0:T(8,128)} %get-tuple-element.22), channel_id=1, source_target_pairs={{1,0},{2,1},{3,2},{4,3},{5,4},{6,5},{7,6},{0,7},{9,8},{10,9},{11,1... | collective-permute-start | bytes 417800 | tf_op jit(solution)/shard_map/ppermute | solution.py:427
  25.0 0.0 collective-permute-done.south_ref
  25.0 0.0 collective-permute-done.1.north_ref
  25.0 0.0 copy-done.6
  25.0 0.0 copy-done.1
  25.0 0.0 copy-done.2
  25.1 0.0 copy-done
  25.1 0.0 copy-start.3
  25.1 1.0 copy-done.3
  26.1 5.5 %shard_map.96 = (f32[10,200,384]{2,1,0:T(8,128)S(1)}, f32[3,200,384]{2,1,0:T(8,128)S(1)}, f32[3,200,384]{2,1,0:T(8,128)S(1)}) custom-call(s32[1]{0:T(128)} %bitcast.k_ref, f32[2,128]{1,0:T(2,128)S(1)} %copy-done.6, f32[2,136,384]{2,1,0:T(8,128)S(1)} %copy-done.3, f32[136,384]{1,0:T(8,128)S(1)} %copy-done.2, f32[2,136,384]{2,1,0:T(8,128)S(1)} %copy-done.1, ...), custom_call_target="tpu_custom_call" | custom-call | flops 30000000 | bytes 7500000 | tf_op jit(solution)/shard_map/pallas_call | solution.py:432
  31.5 0.0 collective-permute-done.2.from_west
  31.5 1.1 collective-permute-done.3.from_east
  32.7 4.5 %collective-permute-start.4 = (f32[64,256]{1,0:T(8,128)S(1)}, f32[64,256]{1,0:T(8,128)S(1)}, u32[]{:S(2)}, u32[]{:S(2)}) collective-permute-start(f32[64,256]{1,0:T(8,128)S(1)} %pad_maximum_fusion), channel_id=1, source_target_pairs={{0,8},{8,16},{16,24},{24,32},{32,40},{40,48},{48,56},{1,9},{9,17},... | collective-permute-start | bytes 196616 | tf_op jit(solution)/shard_map/ppermute | solution.py:446
  37.3 1.9 %collective-permute-start.5 = (f32[64,256]{1,0:T(8,128)S(1)}, f32[64,256]{1,0:T(8,128)S(1)}, u32[]{:S(2)}, u32[]{:S(2)}) collective-permute-start(f32[64,256]{1,0:T(8,128)S(1)} %pad_maximum_fusion.1), channel_id=1, source_target_pairs={{8,0},{16,8},{24,16},{32,24},{40,32},{48,40},{56,48},{9,1},{17,9},... | collective-permute-start | bytes 196616 | tf_op jit(solution)/shard_map/ppermute | solution.py:447
  39.2 0.0 copy-start.4
  39.2 0.0 copy-start.5
  39.2 3.8 %shard_map.97.inner = f32[3,200,384]{2,1,0:T(8,128)S(1)} custom-call(s32[1]{0:T(128)} %bitcast.k_ref, f32[2,128]{1,0:T(2,128)S(1)} %copy-done.6, f32[10,200,384]{2,1,0:T(8,128)S(1)} %get-tuple-element.26.fixed.inner_fixed, f32[3,200,384]{2,1,0:T(8,128)S(1)} %get-tuple-element.27.before, f32[3,200,384]{2,1,0:T(8,128)S(1)} %get-tuple-element.28.gone), custom_call_target="tpu_custom_call" | custom-call | flops 30000000 | bytes 7500000 | tf_op jit(solution)/shard_map/pallas_call | solution.py:441
  43.0 0.0 collective-permute-done.4.corner_south
  43.0 0.0 collective-permute-done.5.corner_north
  43.0 0.0 copy-done.4
  43.0 0.0 copy-done.5
  43.1 5.6 %shard_map.98 = (f32[8,312,128]{2,1,0:T(8,128)S(1)}, f32[10,104,128]{2,1,0:T(8,128)S(1)}, f32[4,72,128]{2,1,0:T(8,128)S(1)}) custom-call(s32[1]{0:T(128)} %bitcast.k_ref, f32[2,128]{1,0:T(2,128)S(1)} %copy-done.6, f32[2,136,384]{2,1,0:T(8,128)S(1)} %copy-done.4, f32[136,384]{1,0:T(8,128)S(1)} %copy-done.2, f32[2,136,384]{2,1,0:T(8,128)S(1)} %copy-done.1, ...), custom_call_target="tpu_custom_call" | custom-call | tf_op jit(solution)/shard_map/pallas_call | solution.py:448
  48.7 41.9 %all_to_all.10.got_ref = f32[8,312,128]{2,1,0:T(8,128)S(1)} all-to-all(f32[8,312,128]{2,1,0:T(8,128)S(1)} %get-tuple-element.29), channel_id=1, replica_groups=mesh['tm'=8,'lat'=8,'lon'=8] {'tm'}, dimensions={0} | all-to-all | bytes 2555904 | tf_op jit(solution)/shard_map/all_to_all | solution.py:463
  90.6 8.6 %shard_map.99 = f32[8,72,384]{2,1,0:T(8,128)S(1)} custom-call(f32[2,128]{1,0:T(2,128)S(1)} %copy-done.6, f32[8,312,128]{2,1,0:T(8,128)S(1)} %all_to_all.10.got_ref, f32[10,104,128]{2,1,0:T(8,128)S(1)} %get-tuple-element.30.fixed, f32[4,72,128]{2,1,0:T(8,128)S(1)} %get-tuple-element.31.flows_ref), custom_call_target="tpu_custom_call" | custom-call | tf_op jit(solution)/shard_map/pallas_call | solution.py:464
  99.1 27.5 %all_to_all.11.got_ref = f32[8,72,384]{2,1,0:T(8,128)S(1)} all-to-all(f32[8,72,384]{2,1,0:T(8,128)S(1)} %shard_map.99), channel_id=1, replica_groups=mesh['tm'=8,'lat'=8,'lon'=8] {'tm'}, dimensions={0} | all-to-all | bytes 1769472 | tf_op jit(solution)/shard_map/all_to_all | solution.py:475
  126.6 1.5 %shard_map.100 = (f32[3,136,384]{2,1,0:T(8,128)}, f32[136,384]{1,0:T(8,128)}) custom-call(f32[8,72,384]{2,1,0:T(8,128)S(1)} %all_to_all.11.got_ref), custom_call_target="tpu_custom_call" | custom-call | tf_op jit(solution)/shard_map/pallas_call | solution.py:476
  (3 shorter events, 0.0 us)
Async XLA Ops:
  0.6 24.4 %copy-start.6 = (f32[2,128]{1,0:T(2,128)S(1)}, f32[2,128]{1,0:T(2,128)}, u32[]{:S(2)}) copy-start(f32[2,128]{1,0:T(2,128)} %constant.11.clone.wave_ref) | copy-start | bytes 3076
  0.6 24.4 %copy-start.1 = (f32[2,136,384]{2,1,0:T(8,128)S(1)}, f32[2,136,384]{2,1,0:T(8,128)}, u32[]{:S(2)}) copy-start(f32[2,136,384]{2,1,0:T(8,128)} %force_ref.3) | copy-start | bytes 1253380
  0.7 24.4 %copy-start.2 = (f32[136,384]{1,0:T(8,128)S(1)}, f32[136,384]{1,0:T(8,128)}, u32[]{:S(2)}) copy-start(f32[136,384]{1,0:T(8,128)} %drag_ref.3) | copy-start | bytes 626692
  0.7 24.4 %copy-start = (f32[1,3,136,384]{3,2,1,0:T(8,128)S(1)}, f32[1,3,136,384]{3,2,1,0:T(8,128)}, u32[]{:S(2)}) copy-start(f32[1,3,136,384]{3,2,1,0:T(8,128)} %param.14) | copy-start | bytes 1880068
  3.6 21.4 %collective-permute-start = (f32[8,32,384]{2,1,0:T(8,128)}, f32[8,32,384]{2,1,0:T(8,128)S(1)}, u32[]{:S(2)}, u32[]{:S(2)}) collective-permute-start(f32[8,32,384]{2,1,0:T(8,128)} %get-tuple-element.19), channel_id=1, source_target_pairs={{0,8},{8,16},{16,24},{24,32},{32,40},{40,48},{48,56},{1,9},{9,17},... | collective-permute-start | bytes 1179656 | tf_op jit(solution)/shard_map/ppermute | solution.py:428
  8.2 16.8 %collective-permute-start.1 = (f32[8,32,384]{2,1,0:T(8,128)}, f32[8,32,384]{2,1,0:T(8,128)S(1)}, u32[]{:S(2)}, u32[]{:S(2)}) collective-permute-start(f32[8,32,384]{2,1,0:T(8,128)} %get-tuple-element.20), channel_id=1, source_target_pairs={{8,0},{16,8},{24,16},{32,24},{40,32},{48,40},{56,48},{9,1},{17,9},... | collective-permute-start | bytes 1179656 | tf_op jit(solution)/shard_map/ppermute | solution.py:429
  13.7 17.9 %collective-permute-start.2 = (f32[136,256]{1,0:T(8,128)}, f32[136,256]{1,0:T(8,128)S(1)}, u32[]{:S(2)}, u32[]{:S(2)}) collective-permute-start(f32[136,256]{1,0:T(8,128)} %get-tuple-element.21), channel_id=1, source_target_pairs={{0,1},{1,2},{2,3},{3,4},{4,5},{5,6},{6,7},{7,0},{8,9},{9,10},{10,1... | collective-permute-start | bytes 417800 | tf_op jit(solution)/shard_map/ppermute | solution.py:426
  16.7 16.0 %collective-permute-start.3 = (f32[136,256]{1,0:T(8,128)}, f32[136,256]{1,0:T(8,128)S(1)}, u32[]{:S(2)}, u32[]{:S(2)}) collective-permute-start(f32[136,256]{1,0:T(8,128)} %get-tuple-element.22), channel_id=1, source_target_pairs={{1,0},{2,1},{3,2},{4,3},{5,4},{6,5},{7,6},{0,7},{9,8},{10,9},{11,1... | collective-permute-start | bytes 417800 | tf_op jit(solution)/shard_map/ppermute | solution.py:427
  25.1 1.0 copy-start.3
  32.7 10.3 %collective-permute-start.4 = (f32[64,256]{1,0:T(8,128)S(1)}, f32[64,256]{1,0:T(8,128)S(1)}, u32[]{:S(2)}, u32[]{:S(2)}) collective-permute-start(f32[64,256]{1,0:T(8,128)S(1)} %pad_maximum_fusion), channel_id=1, source_target_pairs={{0,8},{8,16},{16,24},{24,32},{32,40},{40,48},{48,56},{1,9},{9,17},... | collective-permute-start | bytes 196616 | tf_op jit(solution)/shard_map/ppermute | solution.py:446
  37.3 5.8 %collective-permute-start.5 = (f32[64,256]{1,0:T(8,128)S(1)}, f32[64,256]{1,0:T(8,128)S(1)}, u32[]{:S(2)}, u32[]{:S(2)}) collective-permute-start(f32[64,256]{1,0:T(8,128)S(1)} %pad_maximum_fusion.1), channel_id=1, source_target_pairs={{8,0},{16,8},{24,16},{32,24},{40,32},{48,40},{56,48},{9,1},{17,9},... | collective-permute-start | bytes 196616 | tf_op jit(solution)/shard_map/ppermute | solution.py:447
  39.2 3.8 %copy-start.4 = (f32[2,136,384]{2,1,0:T(8,128)S(1)}, f32[2,136,384]{2,1,0:T(8,128)}, u32[]{:S(2)}) copy-start(f32[2,136,384]{2,1,0:T(8,128)} %get-tuple-element.18.ground_ref) | copy-start | bytes 1253380
  39.2 3.8 %copy-start.5 = (f32[4,136,384]{2,1,0:T(8,128)S(1)}, f32[4,136,384]{2,1,0:T(8,128)}, u32[]{:S(2)}) copy-start(f32[4,136,384]{2,1,0:T(8,128)} %flow_ref.1) | copy-start | bytes 2506756

commit v5 on v4

--- a/solution.py
+++ b/solution.py
@@ -299,7 +299,7 @@
                 old[k, f, at, :] = gain[f] * now
         return carry
 
-    lax.fori_loop(0, CB, start, 0)
+    lax.fori_loop(0, CB, start, 0, unroll=True)
     for i in range(4):
         sums[i] = jnp.zeros((CROWS, 128), F32)
     half = math.sqrt(0.5)

time: 128 us -> 128 us (level)
  no operation moved by 1% of the time
where the time goes in v5:
time: 128 us
  blocking collectives  69.4 us (54%)
  starting transfers between devices  27.8 us (22%)
  Pallas kernels  27.7 us (22%)
    all_to_all x1, blocking collectives, shards(): got = lax.all_to_all(sent, 'tm', 0, 0, tiled=True)  41.9 us
    all_to_all x1, blocking collectives, shards(): home = lax.all_to_all(back, 'tm', 0, 0, tiled=True)  27.5 us
    pallas_call x1, Pallas kernels, shards(): call(last_kernel, ((NTM, OROWS, COLS),), [pltpu.VMEM((NTM, 3, CROWS, 128)...  8.41 us
    ppermute x1, starting transfers between devices, shards(): lax.ppermute(west, 'lon', [((i + 1) % lon_size, i) for i in range(lon_siz...  8.3 us
    pallas_call x1, Pallas kernels, shards(): call(edge_kernel, ((NTM, 3 * CROWS, 128), (10, CROWS, 128), (4, OROWS, 12...  5.64 us
    ppermute x1, starting transfers between devices, shards(): from_north = lax.ppermute(low, 'lat', down)  5.48 us
    pallas_call x1, Pallas kernels, shards(): call(interior_kernel, ((10, EROWS, COLS), deep, deep), [pltpu.VMEM((8, ER...  5.45 us
    ppermute x1, starting transfers between devices, shards(): from_south = lax.ppermute(high, 'lat', up)  4.58 us
  transfers between devices with their start and end apart: 6, of which 1 were waited for; matrix products, arithmetic and copies ran while one was open for 0% of the time, Pallas kernels for 7%

profile of v5, /device:TPU:1, one launch (start us, length us, event | category | flops | bytes accessed | tf_op | source)
XLA Modules:
  0.0 128.0 jit_solution(15732326397395165925)
XLA Ops:
  0.6 0.0 copy-start.6
  0.6 0.0 copy-start.1
  0.7 0.0 copy-start.2
  0.7 0.0 copy-start
  0.7 2.9 %shard_map.95 = (f32[2,136,384]{2,1,0:T(8,128)}, f32[8,32,384]{2,1,0:T(8,128)}, f32[8,32,384]{2,1,0:T(8,128)}, f32[136,256]{1,0:T(8,128)}, f32[136,256]{1,0:T(8,128)}) custom-call(s32[1]{0:T(128)} %bitcast.1.lat_ref, f32[32]{0:T(128)} %levels_hbm.1, s32[136,384]{1,0:T(8,128)} %cls_hbm.1, s32[136,384]{1,0:T(8,128)} %ocean_hbm.1, f32[136,384]{1,0:T(8,128)} %drag_ref.3, ...), custom_call_target="tpu_custom_call" | custom-call | tf_op jit(solution)/shard_map/pallas_call | solution.py:408
  3.6 4.6 %collective-permute-start = (f32[8,32,384]{2,1,0:T(8,128)}, f32[8,32,384]{2,1,0:T(8,128)S(1)}, u32[]{:S(2)}, u32[]{:S(2)}) collective-permute-start(f32[8,32,384]{2,1,0:T(8,128)} %get-tuple-element.19), channel_id=1, source_target_pairs={{0,8},{8,16},{16,24},{24,32},{32,40},{40,48},{48,56},{1,9},{9,17},... | collective-permute-start | bytes 1179656 | tf_op jit(solution)/shard_map/ppermute | solution.py:428
  8.2 5.5 %collective-permute-start.1 = (f32[8,32,384]{2,1,0:T(8,128)}, f32[8,32,384]{2,1,0:T(8,128)S(1)}, u32[]{:S(2)}, u32[]{:S(2)}) collective-permute-start(f32[8,32,384]{2,1,0:T(8,128)} %get-tuple-element.20), channel_id=1, source_target_pairs={{8,0},{16,8},{24,16},{32,24},{40,32},{48,40},{56,48},{9,1},{17,9},... | collective-permute-start | bytes 1179656 | tf_op jit(solution)/shard_map/ppermute | solution.py:429
  13.7 3.0 %collective-permute-start.2 = (f32[136,256]{1,0:T(8,128)}, f32[136,256]{1,0:T(8,128)S(1)}, u32[]{:S(2)}, u32[]{:S(2)}) collective-permute-start(f32[136,256]{1,0:T(8,128)} %get-tuple-element.21), channel_id=1, source_target_pairs={{0,1},{1,2},{2,3},{3,4},{4,5},{5,6},{6,7},{7,0},{8,9},{9,10},{10,1... | collective-permute-start | bytes 417800 | tf_op jit(solution)/shard_map/ppermute | solution.py:426
  16.7 8.3 %collective-permute-start.3 = (f32[136,256]{1,0:T(8,128)}, f32[136,256]{1,0:T(8,128)S(1)}, u32[]{:S(2)}, u32[]{:S(2)}) collective-permute-start(f32[136,256]{1,0:T(8,128)} %get-tuple-element.22), channel_id=1, source_target_pairs={{1,0},{2,1},{3,2},{4,3},{5,4},{6,5},{7,6},{0,7},{9,8},{10,9},{11,1... | collective-permute-start | bytes 417800 | tf_op jit(solution)/shard_map/ppermute | solution.py:427
  25.0 0.0 collective-permute-done.south_ref
  25.0 0.0 collective-permute-done.1.north_ref
  25.0 0.0 copy-done.6
  25.0 0.0 copy-done.1
  25.0 0.0 copy-done.2
  25.1 0.0 copy-done
  25.1 0.0 copy-start.3
  25.1 1.0 copy-done.3
  26.1 5.5 %shard_map.96 = (f32[10,200,384]{2,1,0:T(8,128)S(1)}, f32[3,200,384]{2,1,0:T(8,128)S(1)}, f32[3,200,384]{2,1,0:T(8,128)S(1)}) custom-call(s32[1]{0:T(128)} %bitcast.k_ref, f32[2,128]{1,0:T(2,128)S(1)} %copy-done.6, f32[2,136,384]{2,1,0:T(8,128)S(1)} %copy-done.3, f32[136,384]{1,0:T(8,128)S(1)} %copy-done.2, f32[2,136,384]{2,1,0:T(8,128)S(1)} %copy-done.1, ...), custom_call_target="tpu_custom_call" | custom-call | flops 30000000 | bytes 7500000 | tf_op jit(solution)/shard_map/pallas_call | solution.py:432
  31.5 0.0 collective-permute-done.2.from_west
  31.5 1.1 collective-permute-done.3.from_east
  32.7 4.5 %collective-permute-start.4 = (f32[64,256]{1,0:T(8,128)S(1)}, f32[64,256]{1,0:T(8,128)S(1)}, u32[]{:S(2)}, u32[]{:S(2)}) collective-permute-start(f32[64,256]{1,0:T(8,128)S(1)} %pad_maximum_fusion), channel_id=1, source_target_pairs={{0,8},{8,16},{16,24},{24,32},{32,40},{40,48},{48,56},{1,9},{9,17},... | collective-permute-start | bytes 196616 | tf_op jit(solution)/shard_map/ppermute | solution.py:446
  37.3 1.9 %collective-permute-start.5 = (f32[64,256]{1,0:T(8,128)S(1)}, f32[64,256]{1,0:T(8,128)S(1)}, u32[]{:S(2)}, u32[]{:S(2)}) collective-permute-start(f32[64,256]{1,0:T(8,128)S(1)} %pad_maximum_fusion.1), channel_id=1, source_target_pairs={{8,0},{16,8},{24,16},{32,24},{40,32},{48,40},{56,48},{9,1},{17,9},... | collective-permute-start | bytes 196616 | tf_op jit(solution)/shard_map/ppermute | solution.py:447
  39.2 0.0 copy-start.4
  39.2 0.0 copy-start.5
  39.2 3.8 %shard_map.97.inner = f32[3,200,384]{2,1,0:T(8,128)S(1)} custom-call(s32[1]{0:T(128)} %bitcast.k_ref, f32[2,128]{1,0:T(2,128)S(1)} %copy-done.6, f32[10,200,384]{2,1,0:T(8,128)S(1)} %get-tuple-element.26.fixed.inner_fixed, f32[3,200,384]{2,1,0:T(8,128)S(1)} %get-tuple-element.27.before, f32[3,200,384]{2,1,0:T(8,128)S(1)} %get-tuple-element.28.gone), custom_call_target="tpu_custom_call" | custom-call | flops 30000000 | bytes 7500000 | tf_op jit(solution)/shard_map/pallas_call | solution.py:441
  43.0 0.0 collective-permute-done.4.corner_south
  43.0 0.0 collective-permute-done.5.corner_north
  43.0 0.0 copy-done.4
  43.0 0.0 copy-done.5
  43.1 5.6 %shard_map.98 = (f32[8,312,128]{2,1,0:T(8,128)S(1)}, f32[10,104,128]{2,1,0:T(8,128)S(1)}, f32[4,72,128]{2,1,0:T(8,128)S(1)}) custom-call(s32[1]{0:T(128)} %bitcast.k_ref, f32[2,128]{1,0:T(2,128)S(1)} %copy-done.6, f32[2,136,384]{2,1,0:T(8,128)S(1)} %copy-done.4, f32[136,384]{1,0:T(8,128)S(1)} %copy-done.2, f32[2,136,384]{2,1,0:T(8,128)S(1)} %copy-done.1, ...), custom_call_target="tpu_custom_call" | custom-call | tf_op jit(solution)/shard_map/pallas_call | solution.py:448
  48.7 41.9 %all_to_all.10.got_ref = f32[8,312,128]{2,1,0:T(8,128)S(1)} all-to-all(f32[8,312,128]{2,1,0:T(8,128)S(1)} %get-tuple-element.29), channel_id=1, replica_groups=mesh['tm'=8,'lat'=8,'lon'=8] {'tm'}, dimensions={0} | all-to-all | bytes 2555904 | tf_op jit(solution)/shard_map/all_to_all | solution.py:463
  90.6 8.4 %shard_map.99 = f32[8,72,384]{2,1,0:T(8,128)S(1)} custom-call(f32[2,128]{1,0:T(2,128)S(1)} %copy-done.6, f32[8,312,128]{2,1,0:T(8,128)S(1)} %all_to_all.10.got_ref, f32[10,104,128]{2,1,0:T(8,128)S(1)} %get-tuple-element.30.fixed, f32[4,72,128]{2,1,0:T(8,128)S(1)} %get-tuple-element.31.flows_ref), custom_call_target="tpu_custom_call" | custom-call | tf_op jit(solution)/shard_map/pallas_call | solution.py:464
  99.0 27.5 %all_to_all.11.got_ref = f32[8,72,384]{2,1,0:T(8,128)S(1)} all-to-all(f32[8,72,384]{2,1,0:T(8,128)S(1)} %shard_map.99), channel_id=1, replica_groups=mesh['tm'=8,'lat'=8,'lon'=8] {'tm'}, dimensions={0} | all-to-all | bytes 1769472 | tf_op jit(solution)/shard_map/all_to_all | solution.py:475
  126.5 1.5 %shard_map.100 = (f32[3,136,384]{2,1,0:T(8,128)}, f32[136,384]{1,0:T(8,128)}) custom-call(f32[8,72,384]{2,1,0:T(8,128)S(1)} %all_to_all.11.got_ref), custom_call_target="tpu_custom_call" | custom-call | tf_op jit(solution)/shard_map/pallas_call | solution.py:476
  (3 shorter events, 0.0 us)
Async XLA Ops:
  0.6 24.4 %copy-start.6 = (f32[2,128]{1,0:T(2,128)S(1)}, f32[2,128]{1,0:T(2,128)}, u32[]{:S(2)}) copy-start(f32[2,128]{1,0:T(2,128)} %constant.11.clone.wave_ref) | copy-start | bytes 3076
  0.6 24.4 %copy-start.1 = (f32[2,136,384]{2,1,0:T(8,128)S(1)}, f32[2,136,384]{2,1,0:T(8,128)}, u32[]{:S(2)}) copy-start(f32[2,136,384]{2,1,0:T(8,128)} %force_ref.3) | copy-start | bytes 1253380
  0.7 24.4 %copy-start.2 = (f32[136,384]{1,0:T(8,128)S(1)}, f32[136,384]{1,0:T(8,128)}, u32[]{:S(2)}) copy-start(f32[136,384]{1,0:T(8,128)} %drag_ref.3) | copy-start | bytes 626692
  0.7 24.4 %copy-start = (f32[1,3,136,384]{3,2,1,0:T(8,128)S(1)}, f32[1,3,136,384]{3,2,1,0:T(8,128)}, u32[]{:S(2)}) copy-start(f32[1,3,136,384]{3,2,1,0:T(8,128)} %param.14) | copy-start | bytes 1880068
  3.6 21.4 %collective-permute-start = (f32[8,32,384]{2,1,0:T(8,128)}, f32[8,32,384]{2,1,0:T(8,128)S(1)}, u32[]{:S(2)}, u32[]{:S(2)}) collective-permute-start(f32[8,32,384]{2,1,0:T(8,128)} %get-tuple-element.19), channel_id=1, source_target_pairs={{0,8},{8,16},{16,24},{24,32},{32,40},{40,48},{48,56},{1,9},{9,17},... | collective-permute-start | bytes 1179656 | tf_op jit(solution)/shard_map/ppermute | solution.py:428
  8.2 16.8 %collective-permute-start.1 = (f32[8,32,384]{2,1,0:T(8,128)}, f32[8,32,384]{2,1,0:T(8,128)S(1)}, u32[]{:S(2)}, u32[]{:S(2)}) collective-permute-start(f32[8,32,384]{2,1,0:T(8,128)} %get-tuple-element.20), channel_id=1, source_target_pairs={{8,0},{16,8},{24,16},{32,24},{40,32},{48,40},{56,48},{9,1},{17,9},... | collective-permute-start | bytes 1179656 | tf_op jit(solution)/shard_map/ppermute | solution.py:429
  13.7 17.9 %collective-permute-start.2 = (f32[136,256]{1,0:T(8,128)}, f32[136,256]{1,0:T(8,128)S(1)}, u32[]{:S(2)}, u32[]{:S(2)}) collective-permute-start(f32[136,256]{1,0:T(8,128)} %get-tuple-element.21), channel_id=1, source_target_pairs={{0,1},{1,2},{2,3},{3,4},{4,5},{5,6},{6,7},{7,0},{8,9},{9,10},{10,1... | collective-permute-start | bytes 417800 | tf_op jit(solution)/shard_map/ppermute | solution.py:426
  16.7 16.0 %collective-permute-start.3 = (f32[136,256]{1,0:T(8,128)}, f32[136,256]{1,0:T(8,128)S(1)}, u32[]{:S(2)}, u32[]{:S(2)}) collective-permute-start(f32[136,256]{1,0:T(8,128)} %get-tuple-element.22), channel_id=1, source_target_pairs={{1,0},{2,1},{3,2},{4,3},{5,4},{6,5},{7,6},{0,7},{9,8},{10,9},{11,1... | collective-permute-start | bytes 417800 | tf_op jit(solution)/shard_map/ppermute | solution.py:427
  25.1 1.0 copy-start.3
  32.7 10.3 %collective-permute-start.4 = (f32[64,256]{1,0:T(8,128)S(1)}, f32[64,256]{1,0:T(8,128)S(1)}, u32[]{:S(2)}, u32[]{:S(2)}) collective-permute-start(f32[64,256]{1,0:T(8,128)S(1)} %pad_maximum_fusion), channel_id=1, source_target_pairs={{0,8},{8,16},{16,24},{24,32},{32,40},{40,48},{48,56},{1,9},{9,17},... | collective-permute-start | bytes 196616 | tf_op jit(solution)/shard_map/ppermute | solution.py:446
  37.3 5.8 %collective-permute-start.5 = (f32[64,256]{1,0:T(8,128)S(1)}, f32[64,256]{1,0:T(8,128)S(1)}, u32[]{:S(2)}, u32[]{:S(2)}) collective-permute-start(f32[64,256]{1,0:T(8,128)S(1)} %pad_maximum_fusion.1), channel_id=1, source_target_pairs={{8,0},{16,8},{24,16},{32,24},{40,32},{48,40},{56,48},{9,1},{17,9},... | collective-permute-start | bytes 196616 | tf_op jit(solution)/shard_map/ppermute | solution.py:447
  39.2 3.8 %copy-start.4 = (f32[2,136,384]{2,1,0:T(8,128)S(1)}, f32[2,136,384]{2,1,0:T(8,128)}, u32[]{:S(2)}) copy-start(f32[2,136,384]{2,1,0:T(8,128)} %get-tuple-element.18.ground_ref) | copy-start | bytes 1253380
  39.2 3.8 %copy-start.5 = (f32[4,136,384]{2,1,0:T(8,128)S(1)}, f32[4,136,384]{2,1,0:T(8,128)}, u32[]{:S(2)}) copy-start(f32[4,136,384]{2,1,0:T(8,128)} %flow_ref.1) | copy-start | bytes 2506756
